TPU v7x, 256 devices: a whole 4x4x8 slice. The times are simulated.
256 devices in a mesh: tm: 4 (over x_lo, core), freq: 64 (over y, x_hi, z).
Axes of the slice: x: 4 (x_hi: 2, x_lo: 2; x = x_hi * 2 + x_lo), y: 4, z: 8, core: 2. Of those that a mesh axis runs over, the one named last changes fastest.
Arguments:
- visibilities: float32 [2, 4, 32, 64, 2016], P(None, None, 'tm', 'freq'), may hold values from -48 to 48
- sky_model: float32 [2, 4, 32, 64, 2016], P(None, None, 'tm', 'freq'), may hold values from -3 to 3
- gain_time: float32 [2, 2, 8, 64], P(None, None, 'tm'), may hold values from -4 to 4
- gain_band: float32 [2, 2, 64, 64], P(None, None, 'freq'), may hold values from -2.5 to 2.5
- delay_start: float32 [2, 64], replicated, may hold values from -2.2 to 2.2
- first_antenna: int32 [2016], replicated, may hold values from 0 to 63, as said below
- second_antenna: int32 [2016], replicated, may hold values from 0 to 63
Outputs:
- solved_time: float32 [2, 2, 8, 64], P(None, None, 'tm')
- solved_band: float32 [2, 2, 64, 64], P(None, None, 'freq')
- solved_delay: float32 [2, 64], replicated
- weights: float32 [32, 2016], P('tm')
- residual: float32 [2, 4, 32, 64, 2016], P(None, None, 'tm', 'freq')
Inputs may be any that keep to these rules, and one draw needn't show every extreme that they name: first_antenna and second_antenna together name every unordered pair of distinct antennas of the 64 exactly once, in an order and orientation drawn from the seed.
All inputs are finite; a program needn't handle non-finite values.
Results may differ from a plain program's by a relative error of at most 0.00013.
Values sent between devices are 32-bit elements; how exact they have to be, the bound alone decides.
No kernel may reach another device: no remote copies, remote signals or barrier semaphores. Data moves between devices by JAX's collectives and lax.ppermute only.
A program may use at most 64 MiB of HBM per device.

v0:
```python
import functools
import math

import jax
import jax.numpy as jnp
from jax import lax
from jax.experimental import pallas as pl
from jax.experimental.pallas import tpu as pltpu
from jax.sharding import Mesh
from jax.sharding import PartitionSpec as P

SWEEPS = 2
TURN = 2.0 * math.pi
DAMPING = 0.5
EPSILON = 1e-06
LANES = 128
HALF = 64
FREQ = ("freq_0", "freq_1", "freq_2")
TM = ("tm_0", "tm_1")
F32 = jnp.float32


def rows_of(array, start, count):
    return array[start : start + count]


def half_roll(array):
    return pltpu.roll(array, HALF, 1)


def low_half(shape):
    return lax.broadcasted_iota(jnp.int32, shape, 1) < HALF


def cmul(ar, ai, br, bi):
    return ar * br - ai * bi, ar * bi + ai * br


def conj_mul(ar, ai, br, bi):
    return ar * br + ai * bi, ar * bi - ai * br


def chain(gain, band, delay, x):
    angle = TURN * delay * x
    kr, ki = jnp.cos(angle), jnp.sin(angle)
    hr, hi = cmul(band[0:2], band[2:4], kr, ki)
    gr, gi = cmul(gain[0:2], gain[2:4], hr, hi)
    return (kr, ki), (hr, hi), (gr, gi)


def fill(row):
    return jnp.broadcast_to(row, (8, LANES))


def index_rows(index_ref, side, block, offset):
    row = index_ref[side : side + 1, block * LANES : (block + 1) * LANES]
    return fill(row) + offset


def lookup(source, index):
    return jnp.take_along_axis(source, index, axis=1)


def residual_blocks(v_ref, s_ref, index_ref, gr, gi):
    offset = jnp.where(lax.broadcasted_iota(jnp.int32, (8, LANES), 0) >= 4, HALF, 0)
    sources = [(fill(gr[a : a + 1]), fill(gi[a : a + 1])) for a in range(2)]
    blocks = v_ref.shape[1] // LANES
    for block in range(blocks):
        lanes = pl.ds(block * LANES, LANES)
        first = index_rows(index_ref, 0, block, offset)
        second = index_rows(index_ref, 1, block, offset)
        left = [(lookup(re, first), lookup(im, first)) for re, im in sources]
        right = [(lookup(re, second), lookup(im, second)) for re, im in sources]
        for c in range(4):
            (pr, pi), (qr, qi) = left[c // 2], right[c % 2]
            cr, ci = pr * qr + pi * qi, pi * qr - pr * qi
            sr = s_ref[pl.ds(c * 8, 8), lanes]
            si = s_ref[pl.ds(32 + c * 8, 8), lanes]
            mr, mi = cmul(cr, ci, sr, si)
            yield (
                block,
                c,
                v_ref[pl.ds(c * 8, 8), lanes] - mr,
                v_ref[pl.ds(32 + c * 8, 8), lanes] - mi,
            )


def noise_into(v_ref, s_ref, index_ref, gr, gi, power_ref):
    for block, c, rr, ri in residual_blocks(v_ref, s_ref, index_ref, gr, gi):
        term = rr * rr + ri * ri
        total = term if c == 0 else total + term
        if c == 3:
            power_ref[pl.ds(block * 8, 8), :] = total


def fold_rows(ref, count, group):
    whole = group if group % 8 == 0 else math.lcm(group, 8)
    value = jnp.sum(ref[...].reshape(count * group // whole, whole, LANES), axis=0)
    while whole > group and group % 2:
        break
    if whole == group:
        return value
    total = value[0:group]
    for at in range(group, whole, group):
        total = total + value[at : at + group]
    return total


def delay_step(received_ref, delay):
    summed = fold_rows(received_ref, 64, 2)
    step = DAMPING * summed[0:1] / summed[1:2]
    low = low_half((1, LANES))
    turned = half_roll(jnp.broadcast_to(step, (8, LANES)))[0:1]
    both = jnp.concatenate([jnp.where(low, step, turned), jnp.where(low, turned, step)], axis=0)
    return delay + both


def first_kernel(v_ref, s_ref, index_ref, gain_ref, band_ref, delay_ref, x_ref, power_ref):
    _, _, (gr, gi) = chain(gain_ref[...], band_ref[...], delay_ref[...], x_ref[0, 0])
    noise_into(v_ref, s_ref, index_ref, gr, gi, power_ref)


def next_kernel(
    v_ref, s_ref, index_ref, gain_ref, band_ref, delay_ref, received_ref, x_ref, power_ref, new_ref
):
    delay = delay_step(received_ref, delay_ref[...])
    new_ref[...] = delay
    _, _, (gr, gi) = chain(gain_ref[...], band_ref[...], delay, x_ref[0, 0])
    noise_into(v_ref, s_ref, index_ref, gr, gi, power_ref)


def last_kernel(
    v_ref, s_ref, index_ref, gain_ref, band_ref, delay_ref, received_ref, x_ref, out_ref, new_ref
):
    delay = delay_step(received_ref, delay_ref[...])
    new_ref[...] = delay
    _, _, (gr, gi) = chain(gain_ref[...], band_ref[...], delay, x_ref[0, 0])
    for block, c, rr, ri in residual_blocks(v_ref, s_ref, index_ref, gr, gi):
        lanes = pl.ds(block * LANES, LANES)
        out_ref[pl.ds(c * 8, 8), lanes] = rr
        out_ref[pl.ds(32 + c * 8, 8), lanes] = ri


def weight_kernel(scale, parts_ref, out_ref):
    summed = jnp.sum(parts_ref[...].reshape(16, 8, LANES), axis=0)
    summed = summed[0:2] + summed[2:4] + (summed[4:6] + summed[6:8])
    weight = 1.0 / (summed * scale + EPSILON)
    eight = jnp.concatenate([weight] * 4, axis=0)
    for at in range(16):
        out_ref[pl.ds(at * 8, 8), :] = eight


def normal_sums(load_stats, blocks, index_ref, hot_ref, gr, gi, left_ref):
    row = lax.broadcasted_iota(jnp.int32, (8, LANES), 0)
    offset = (row % 2) * HALF
    top = row < 4
    inner = (row // 2) % 2 == 0

    def pick(mask, part):
        return jnp.where(mask, fill(part[0:1]), fill(part[1:2]))

    p_re, p_im = pick(top, gr), pick(top, gi)
    q_re, q_im = pick(inner, gr), pick(inner, gi)
    for block in range(blocks):
        lanes = pl.ds(block * LANES, LANES)
        first = index_rows(index_ref, 0, block, offset)
        second = index_rows(index_ref, 1, block, offset)
        pr, pi = lookup(p_re, first), lookup(p_im, first)
        qr, qi = lookup(q_re, second), lookup(q_im, second)
        cr, ci, power = load_stats(block)
        rr = cr - (pr * qr + pi * qi) * power
        ri = ci - (pi * qr - pr * qi) * power
        terms = jnp.concatenate(
            [
                qr * rr - qi * ri,
                qr * ri + qi * rr,
                (qr * qr + qi * qi) * power,
                pr * rr + pi * ri,
                pi * rr - pr * ri,
                (pr * pr + pi * pi) * power,
            ],
            axis=0,
        )
        high = terms.astype(jnp.bfloat16)
        rest = terms - high.astype(F32)
        middle = rest.astype(jnp.bfloat16)
        low = (rest - middle.astype(F32)).astype(jnp.bfloat16)
        left_ref[0:48, lanes] = high
        left_ref[48:96, lanes] = middle
        left_ref[96:144, lanes] = low
    sums = jnp.dot(left_ref[...], hot_ref[...], preferred_element_type=F32)
    sums = sums[0:48] + (sums[48:96] + sums[96:144])
    turned = half_roll(sums)
    low_lanes = low_half((1, LANES))
    out = []
    for kind in range(3):
        made = []
        for a in range(2):
            p, q = kind * 8 + 4 * a, 24 + kind * 8 + 2 * a

            def at(array, index):
                return array[index : index + 1]

            here = at(sums, p) + at(sums, p + 2) + (at(turned, q) + at(turned, q + 4))
            there = at(turned, p + 1) + at(turned, p + 3) + (at(sums, q + 1) + at(sums, q + 5))
            made.append(jnp.where(low_lanes, here, there))
        out.append(jnp.concatenate(made, axis=0))
    return out


def stats_loader(stats_ref):
    def load(block):
        lanes = pl.ds(block * LANES, LANES)
        return stats_ref[0:8, lanes], stats_ref[8:16, lanes], stats_ref[16:24, lanes]

    return load


def time_kernel(
    v_ref,
    s_ref,
    weight_ref,
    index_ref,
    hot_ref,
    gain_ref,
    band_ref,
    delay_ref,
    x_ref,
    stats_ref,
    send_ref,
    real_ref,
    imag_ref,
    power_ref,
    left_ref,
):
    blocks = v_ref.shape[1] // LANES
    for block in range(blocks):
        lanes = pl.ds(block * LANES, LANES)
        weight = weight_ref[pl.ds(block * 8, 8), :]
        for c in range(4):
            sr, si = s_ref[pl.ds(c * 8, 8), lanes], s_ref[pl.ds(32 + c * 8, 8), lanes]
            vr, vi = v_ref[pl.ds(c * 8, 8), lanes], v_ref[pl.ds(32 + c * 8, 8), lanes]
            xr, xi = conj_mul(sr, si, vr, vi)
            rows = pl.ds(block * 32 + c * 8, 8)
            real_ref[rows, :] = weight * xr
            imag_ref[rows, :] = weight * xi
            power_ref[rows, :] = weight * (sr * sr + si * si)
        for slot, ref in enumerate((real_ref, imag_ref, power_ref)):
            parts = [ref[pl.ds(block * 32 + t, 8, stride=4), :] for t in range(4)]
            stats_ref[slot * 8 : slot * 8 + 8, lanes] = parts[0] + parts[1] + (parts[2] + parts[3])
    _, (hr, hi), (gr, gi) = chain(gain_ref[...], band_ref[...], delay_ref[...], x_ref[0, 0])
    ur, ui, w = normal_sums(stats_loader(stats_ref), blocks, index_ref, hot_ref, gr, gi, left_ref)
    nr, ni = conj_mul(hr, hi, ur, ui)
    packed = jnp.concatenate([nr, ni, (hr * hr + hi * hi) * w], axis=0)
    repeated = jnp.concatenate([packed] * 4, axis=0)
    for at in range(16):
        send_ref[pl.ds(at * 24, 24), :] = repeated


def stepped(numerator_re, numerator_im, denominator):
    return jnp.concatenate(
        [DAMPING * numerator_re / denominator, DAMPING * numerator_im / denominator], axis=0
    )


def band_kernel(
    stats_ref,
    received_ref,
    index_ref,
    hot_ref,
    gain_ref,
    band_ref,
    delay_ref,
    x_ref,
    new_ref,
    send_ref,
    left_ref,
):
    summed = fold_rows(received_ref, 64, 6)
    gain = gain_ref[...] + stepped(summed[0:2], summed[2:4], summed[4:6])
    new_ref[...] = gain
    (kr, ki), _, (gr, gi) = chain(gain, band_ref[...], delay_ref[...], x_ref[0, 0])
    blocks = stats_ref.shape[1] // LANES
    ur, ui, w = normal_sums(stats_loader(stats_ref), blocks, index_ref, hot_ref, gr, gi, left_ref)
    hr, hi = cmul(gain[0:2], gain[2:4], kr, ki)
    nr, ni = conj_mul(hr, hi, ur, ui)
    packed = jnp.concatenate(
        [nr, ni, (hr * hr + hi * hi) * w, jnp.zeros((2, LANES), F32)], axis=0
    )
    send_ref[...] = packed + half_roll(packed)


def delay_kernel(
    stats_ref,
    received_ref,
    index_ref,
    hot_ref,
    gain_ref,
    band_ref,
    delay_ref,
    x_ref,
    new_ref,
    send_ref,
    left_ref,
):
    summed = received_ref[...]
    band = band_ref[...] + stepped(summed[0:2], summed[2:4], summed[4:6])
    new_ref[...] = band
    x = x_ref[0, 0]
    _, _, (gr, gi) = chain(gain_ref[...], band, delay_ref[...], x)
    blocks = stats_ref.shape[1] // LANES
    ur, ui, w = normal_sums(stats_loader(stats_ref), blocks, index_ref, hot_ref, gr, gi, left_ref)
    turning = TURN * x
    n = turning * (gr * ui - gi * ur)
    d = (turning * turning) * ((gr * gr + gi * gi) * w)
    packed = jnp.concatenate([n, d, jnp.zeros((4, LANES), F32)], axis=0)
    packed = packed + half_roll(packed)
    low = low_half((1, LANES))
    pair = jnp.concatenate(
        [jnp.where(low, packed[0:1], packed[1:2]), jnp.where(low, packed[2:3], packed[3:4])],
        axis=0,
    )
    send_ref[...] = jnp.concatenate([pair] * 4, axis=0)


def call(body, outs, operands, scratch=()):
    vmem = pl.BlockSpec(memory_space=pltpu.VMEM)
    smem = pl.BlockSpec(memory_space=pltpu.SMEM)
    return pl.pallas_call(
        body,
        out_shape=tuple(jax.ShapeDtypeStruct(o, F32) for o in outs),
        in_specs=[smem if o.shape == (1, 1) else vmem for o in operands],
        out_specs=tuple(vmem for _ in outs),
        scratch_shapes=list(scratch),
        compiler_params=pltpu.CompilerParams(vmem_limit_bytes=12 << 20),
    )(*operands)


def exchange(array):
    devices = lax.axis_size(FREQ)
    chunks = array.reshape(devices, 1, -1)
    return lax.all_to_all(chunks, FREQ, 0, 0, tiled=True).reshape(array.shape)


def pair_total(array):
    for axis in ("tm_1", "tm_0"):
        array = array + lax.ppermute(array, axis, [(0, 1), (1, 0)])
    return array


def shards(
    visibilities, sky_model, gain_time, gain_band, delay_start, first_antenna, second_antenna
):
    antennas = gain_time.shape[-1]
    baselines = visibilities.shape[4]
    padded = -(-baselines // LANES) * LANES
    times = visibilities.shape[2]
    channels = lax.axis_size(FREQ)
    x = (lax.axis_index(FREQ).astype(F32) + 0.5) / channels - 0.5
    x = x.reshape(1, 1)

    def plane(array):
        flat = array.reshape(-1, baselines)
        return jnp.pad(flat, ((0, 0), (0, padded - baselines)))

    v, s = plane(visibilities), plane(sky_model)
    ids = jnp.stack([first_antenna, second_antenna])
    index = jnp.pad(ids, ((0, 6), (0, padded - baselines)))
    marked = jnp.pad(ids, ((0, 0), (0, padded - baselines)), constant_values=-1)
    hot = jnp.concatenate(
        [marked[k][:, None] == jnp.arange(antennas, dtype=jnp.int32)[None] for k in range(2)],
        axis=1,
    ).astype(jnp.bfloat16)

    gain = gain_time.reshape(4, LANES)
    band = gain_band.reshape(4, antennas)
    band = jnp.concatenate([band, band], axis=1)
    delay = jnp.concatenate([delay_start, delay_start], axis=1)

    left = pltpu.VMEM((144, padded), jnp.bfloat16)
    tall = pltpu.VMEM((padded // LANES * 32, LANES), F32)
    square = (padded // LANES * 8, LANES)
    received = None
    for sweep in range(SWEEPS):
        if sweep == 0:
            (power,) = call(first_kernel, [square], (v, s, index, gain, band, delay, x))
        else:
            power, delay = call(
                next_kernel, [square, delay.shape], (v, s, index, gain, band, delay, received, x)
            )
        (mine,) = call(
            functools.partial(weight_kernel, 1.0 / (4 * channels)), [square], (exchange(power),)
        )
        weight = exchange(mine)
        stats, send = call(
            time_kernel,
            [(24, padded), (384, LANES)],
            (v, s, weight, index, hot, gain, band, delay, x),
            (tall, tall, tall, left),
        )
        gain, send = call(
            band_kernel,
            [gain.shape, (8, LANES)],
            (stats, exchange(send), index, hot, gain, band, delay, x),
            (left,),
        )
        band, send = call(
            delay_kernel,
            [band.shape, (8, LANES)],
            (stats, pair_total(send), index, hot, gain, band, delay, x),
            (left,),
        )
        summed = pair_total(send)
        received = exchange(jnp.broadcast_to(summed[None], (16, 8, LANES)).reshape(128, LANES))
    residual, delay = call(
        last_kernel, [v.shape, delay.shape], (v, s, index, gain, band, delay, received, x)
    )
    weights = weight.reshape(-1, times, LANES).transpose(1, 0, 2).reshape(times, padded)
    return (
        gain.reshape(gain_time.shape),
        band[:, :antennas].reshape(gain_band.shape),
        delay[:, :antennas],
        weights[:, :baselines],
        residual[:, :baselines].reshape(visibilities.shape),
    )


def solution(mesh):
    split = Mesh(
        mesh.devices.reshape(2, 2, 4, 2, 8), ("tm_0", "tm_1", "freq_0", "freq_1", "freq_2")
    )
    placed = (
        P(None, None, TM, FREQ, None),
        P(None, None, TM, FREQ, None),
        P(None, None, TM, None),
        P(None, None, FREQ, None),
        P(),
        P(),
        P(),
    )
    return jax.shard_map(
        shards,
        mesh=split,
        in_specs=placed,
        out_specs=(
            P(None, None, TM, None),
            P(None, None, FREQ, None),
            P(),
            P(TM, None),
            P(None, None, TM, FREQ, None),
        ),
        check_vma=False,
    )
```

profile of v0, /device:TPU:2, one launch (start us, length us, event | category | flops | bytes accessed | tf_op | source)
XLA Modules:
  0.0 174.9 jit_solution(14761398424905964046)
XLA Ops:
  2.1 1.3 copy.22
  5.4 13.7 %all-to-all-start = ((f32[64,1,256]{2,1,0:T(1,128)}), f32[64,1,256]{2,1,0:T(1,128)S(1)}, u32[]{:S(2)}, u32[]{:S(2)}) async-start(f32[64,1,256]{2,1,0:T(1,128)} %bitcast.4), calls=%async_computation | async-start | bytes 131072 | tf_op jit(solution)/shard_map/all_to_all | solution.py:342
  19.1 1.2 iota_compare_fusion
  20.3 10.9 %all-to-all-done = f32[64,1,256]{2,1,0:T(1,128)S(1)} async-done(((f32[64,1,256]{2,1,0:T(1,128)}), f32[64,1,256]{2,1,0:T(1,128)S(1)}, u32[]{:S(2)}, u32[]{:S(2)}) %all-to-all-start) | async-done | bytes 65568 | tf_op jit(solution)/shard_map/all_to_all | solution.py:342
  31.9 4.6 %all-to-all-start.1 = ((f32[64,1,256]{2,1,0:T(1,128)}), f32[64,1,256]{2,1,0:T(1,128)S(1)}, u32[]{:S(2)}, u32[]{:S(2)}) async-start(f32[64,1,256]{2,1,0:T(1,128)} %bitcast.6), calls=%async_computation.1 | async-start | bytes 131072 | tf_op jit(solution)/shard_map/all_to_all | solution.py:342
  36.8 11.8 %all-to-all-done.1 = f32[64,1,256]{2,1,0:T(1,128)S(1)} async-done(((f32[64,1,256]{2,1,0:T(1,128)}), f32[64,1,256]{2,1,0:T(1,128)S(1)}, u32[]{:S(2)}, u32[]{:S(2)}) %all-to-all-start.1) | async-done | bytes 65568 | tf_op jit(solution)/shard_map/all_to_all | solution.py:342
  49.4 17.0 %all_to_all.40 = f32[64,1,768]{2,1,0:T(1,128)S(1)} all-to-all(f32[64,1,768]{2,1,0:T(1,128)S(1)} %bitcast.48), channel_id=1, replica_groups=mesh['tm_0'=2,'tm_1'=2,'freq_0'=4,'freq_1'=2,'freq_2'=8] {'freq_0','freq..., dimensions={0} | all-to-all | bytes 393216 | tf_op jit(solution)/shard_map/all_to_all | solution.py:342
  67.1 1.2 collective-permute-done
  68.3 1.4 collective-permute-start.1
  69.7 2.2 %collective-permute-done.1 = f32[8,128]{1,0:T(8,128)S(1)} collective-permute-done((f32[8,128]{1,0:T(8,128)S(1)}, f32[8,128]{1,0:T(8,128)S(1)}, u32[]{:S(2)}, u32[]{:S(2)}) %collective-permute-start.1) | collective-permute-done | bytes 4128 | tf_op jit(solution)/shard_map/ppermute | solution.py:347
  72.6 1.2 collective-permute-done.2
  73.7 1.4 collective-permute-start.3
  75.2 2.2 %collective-permute-done.3 = f32[8,128]{1,0:T(8,128)S(1)} collective-permute-done((f32[8,128]{1,0:T(8,128)S(1)}, f32[8,128]{1,0:T(8,128)S(1)}, u32[]{:S(2)}, u32[]{:S(2)}) %collective-permute-start.3) | collective-permute-done | bytes 4128 | tf_op jit(solution)/shard_map/ppermute | solution.py:347
  77.4 16.3 %all_to_all.41 = f32[64,1,256]{2,1,0:T(1,128)S(1)} all-to-all(f32[64,1,256]{2,1,0:T(1,128)S(1)} %bitcast.54), channel_id=1, replica_groups=mesh['tm_0'=2,'tm_1'=2,'freq_0'=4,'freq_1'=2,'freq_2'=8] {'freq_0','freq..., dimensions={0} | all-to-all | bytes 131072 | tf_op jit(solution)/shard_map/all_to_all | solution.py:342
  94.2 16.0 %all_to_all.42 = f32[64,1,256]{2,1,0:T(1,128)S(1)} all-to-all(f32[64,1,256]{2,1,0:T(1,128)S(1)} %bitcast.50), channel_id=1, replica_groups=mesh['tm_0'=2,'tm_1'=2,'freq_0'=4,'freq_1'=2,'freq_2'=8] {'freq_0','freq..., dimensions={0} | all-to-all | bytes 131072 | tf_op jit(solution)/shard_map/all_to_all | solution.py:342
  110.2 15.9 %all_to_all.43 = f32[64,1,256]{2,1,0:T(1,128)S(1)} all-to-all(f32[64,1,256]{2,1,0:T(1,128)S(1)} %bitcast.47), channel_id=1, replica_groups=mesh['tm_0'=2,'tm_1'=2,'freq_0'=4,'freq_1'=2,'freq_2'=8] {'freq_0','freq..., dimensions={0} | all-to-all | bytes 131072 | tf_op jit(solution)/shard_map/all_to_all | solution.py:342
  126.9 16.9 %all_to_all.44 = f32[64,1,768]{2,1,0:T(1,128)S(1)} all-to-all(f32[64,1,768]{2,1,0:T(1,128)S(1)} %bitcast.49), channel_id=1, replica_groups=mesh['tm_0'=2,'tm_1'=2,'freq_0'=4,'freq_1'=2,'freq_2'=8] {'freq_0','freq..., dimensions={0} | all-to-all | bytes 393216 | tf_op jit(solution)/shard_map/all_to_all | solution.py:342
  145.7 1.4 collective-permute-start.5
  147.1 2.2 %collective-permute-done.5 = f32[8,128]{1,0:T(8,128)S(1)} collective-permute-done((f32[8,128]{1,0:T(8,128)S(1)}, f32[8,128]{1,0:T(8,128)S(1)}, u32[]{:S(2)}, u32[]{:S(2)}) %collective-permute-start.5) | collective-permute-done | bytes 4128 | tf_op jit(solution)/shard_map/ppermute | solution.py:347
  151.2 1.4 collective-permute-start.7
  152.6 2.2 %collective-permute-done.7 = f32[8,128]{1,0:T(8,128)S(1)} collective-permute-done((f32[8,128]{1,0:T(8,128)S(1)}, f32[8,128]{1,0:T(8,128)S(1)}, u32[]{:S(2)}, u32[]{:S(2)}) %collective-permute-start.7) | collective-permute-done | bytes 4128 | tf_op jit(solution)/shard_map/ppermute | solution.py:347
  155.4 4.6 %all-to-all-start.7 = ((f32[64,1,256]{2,1,0:T(1,128)}), f32[64,1,256]{2,1,0:T(1,128)S(1)}, u32[]{:S(2)}, u32[]{:S(2)}) async-start(f32[64,1,256]{2,1,0:T(1,128)} %bitcast.22), calls=%async_computation.7 | async-start | bytes 131072 | tf_op jit(solution)/shard_map/all_to_all | solution.py:342
  160.7 11.5 %all-to-all-done.7 = f32[64,1,256]{2,1,0:T(1,128)S(1)} async-done(((f32[64,1,256]{2,1,0:T(1,128)}), f32[64,1,256]{2,1,0:T(1,128)S(1)}, u32[]{:S(2)}, u32[]{:S(2)}) %all-to-all-start.7) | async-done | bytes 65568 | tf_op jit(solution)/shard_map/all_to_all | solution.py:342
  172.9 1.3 copy.21
  (53 shorter events, 14.2 us)
Async XLA Ops:
  0.6 0.7 copy-start.6
  0.7 0.7 copy-start.5
  1.3 0.7 copy-start.4
  2.1 1.3 copy-start.1
  3.6 0.7 copy-start.3
  3.6 0.7 copy-start.2
  5.4 25.8 %all-to-all-start = ((f32[64,1,256]{2,1,0:T(1,128)}), f32[64,1,256]{2,1,0:T(1,128)S(1)}, u32[]{:S(2)}, u32[]{:S(2)}) async-start(f32[64,1,256]{2,1,0:T(1,128)} %bitcast.4), calls=%async_computation | async-start | bytes 131072 | tf_op jit(solution)/shard_map/all_to_all | solution.py:342
  31.9 16.8 %all-to-all-start.1 = ((f32[64,1,256]{2,1,0:T(1,128)}), f32[64,1,256]{2,1,0:T(1,128)S(1)}, u32[]{:S(2)}, u32[]{:S(2)}) async-start(f32[64,1,256]{2,1,0:T(1,128)} %bitcast.6), calls=%async_computation.1 | async-start | bytes 131072 | tf_op jit(solution)/shard_map/all_to_all | solution.py:342
  67.1 1.2 collective-permute-start
  68.3 3.6 %collective-permute-start.1 = (f32[8,128]{1,0:T(8,128)S(1)}, f32[8,128]{1,0:T(8,128)S(1)}, u32[]{:S(2)}, u32[]{:S(2)}) collective-permute-start(f32[8,128]{1,0:T(8,128)S(1)} %add.45), channel_id=1, source_target_pairs={{0,128},{128,0},{1,129},{129,1},{2,130},{130,2},{3,131},{131,3},{4... | collective-permute-start | bytes 12296 | tf_op jit(solution)/shard_map/ppermute | solution.py:347
  72.5 1.2 collective-permute-start.2
  73.7 3.6 %collective-permute-start.3 = (f32[8,128]{1,0:T(8,128)S(1)}, f32[8,128]{1,0:T(8,128)S(1)}, u32[]{:S(2)}, u32[]{:S(2)}) collective-permute-start(f32[8,128]{1,0:T(8,128)S(1)} %add.47), channel_id=1, source_target_pairs={{0,128},{128,0},{1,129},{129,1},{2,130},{130,2},{3,131},{131,3},{4... | collective-permute-start | bytes 12296 | tf_op jit(solution)/shard_map/ppermute | solution.py:347
  144.5 1.2 collective-permute-start.4
  145.7 3.6 %collective-permute-start.5 = (f32[8,128]{1,0:T(8,128)S(1)}, f32[8,128]{1,0:T(8,128)S(1)}, u32[]{:S(2)}, u32[]{:S(2)}) collective-permute-start(f32[8,128]{1,0:T(8,128)S(1)} %add.49), channel_id=1, source_target_pairs={{0,128},{128,0},{1,129},{129,1},{2,130},{130,2},{3,131},{131,3},{4... | collective-permute-start | bytes 12296 | tf_op jit(solution)/shard_map/ppermute | solution.py:347
  150.0 1.2 collective-permute-start.6
  151.2 3.6 %collective-permute-start.7 = (f32[8,128]{1,0:T(8,128)S(1)}, f32[8,128]{1,0:T(8,128)S(1)}, u32[]{:S(2)}, u32[]{:S(2)}) collective-permute-start(f32[8,128]{1,0:T(8,128)S(1)} %add.51), channel_id=1, source_target_pairs={{0,128},{128,0},{1,129},{129,1},{2,130},{130,2},{3,131},{131,3},{4... | collective-permute-start | bytes 12296 | tf_op jit(solution)/shard_map/ppermute | solution.py:347
  155.4 16.8 %all-to-all-start.7 = ((f32[64,1,256]{2,1,0:T(1,128)}), f32[64,1,256]{2,1,0:T(1,128)S(1)}, u32[]{:S(2)}, u32[]{:S(2)}) async-start(f32[64,1,256]{2,1,0:T(1,128)} %bitcast.22), calls=%async_computation.7 | async-start | bytes 131072 | tf_op jit(solution)/shard_map/all_to_all | solution.py:342
  160.7 11.5 %copy-start = (f32[4,128]{1,0:T(4,128)S(1)}, f32[4,128]{1,0:T(4,128)}, u32[]{:S(2)}) copy-start(f32[4,128]{1,0:T(4,128)} %get-tuple-element.33.band_ref) | copy-start | bytes 6148
where the time goes:
time: 175 us
  blocking collectives  82.1 us (47%)
  waiting for transfers between devices  47.5 us (27%)
  starting transfers between devices  28.8 us (16%)
  Pallas kernels  7.07 us (4%)
  local copies, waits for them, and re-layouts  6.78 us (4%)
  other arithmetic  1.76 us (1%)
    all_to_all x5, blocking collectives, exchange(): return lax.all_to_all(chunks, FREQ, 0, 0, tiled=True).reshape(array.shape)  82.1 us
    all_to_all x3, waiting for transfers between devices, exchange(): return lax.all_to_all(chunks, FREQ, 0, 0, tiled=True).reshape(array.shape)  34.2 us
    all_to_all x3, starting transfers between devices, exchange(): return lax.all_to_all(chunks, FREQ, 0, 0, tiled=True).reshape(array.shape)  22.9 us
    ppermute x8, waiting for transfers between devices, pair_total(): array = array + lax.ppermute(array, axis, [(0, 1), (1, 0)])  13.3 us
    pallas_call x11, Pallas kernels, call(): pl.pallas_call(body, out_shape=tuple((jax.ShapeDtypeStruct(o, F32) for o...  7.07 us
    ppermute x8, starting transfers between devices, pair_total(): array = array + lax.ppermute(array, axis, [(0, 1), (1, 0)])  5.87 us
    unnamed x18, local copies, waits for them, and re-layouts  5.28 us
  transfers between devices with their start and end apart: 11, of which 11 were waited for; matrix products, arithmetic and copies ran while one was open for 1% of the time, Pallas kernels for 0%

commit v1 on v0

v1 whole, which is shorter than its diff:
```python
import functools
import math

import jax
import jax.numpy as jnp
from jax import lax
from jax.experimental import pallas as pl
from jax.experimental.pallas import tpu as pltpu
from jax.sharding import Mesh
from jax.sharding import PartitionSpec as P

SWEEPS = 2
TURN = 2.0 * math.pi
DAMPING = 0.5
EPSILON = 1e-06
LANES = 128
HALF = 64
FREQ = ("freq_0", "freq_1", "freq_2")
TM = ("tm_0", "tm_1")
YX = ("freq_0", "freq_1")
Z = "freq_2"
F32 = jnp.float32


def half_roll(array):
    return pltpu.roll(array, HALF, 1)


def low_half(shape):
    return lax.broadcasted_iota(jnp.int32, shape, 1) < HALF


def cmul(ar, ai, br, bi):
    return ar * br - ai * bi, ar * bi + ai * br


def conj_mul(ar, ai, br, bi):
    return ar * br + ai * bi, ar * bi - ai * br


def chain(gain, band, delay, x):
    angle = TURN * delay * x
    kr, ki = jnp.cos(angle), jnp.sin(angle)
    hr, hi = cmul(band[0:2], band[2:4], kr, ki)
    gr, gi = cmul(gain[0:2], gain[2:4], hr, hi)
    return (kr, ki), (hr, hi), (gr, gi)


def fill(row):
    return jnp.broadcast_to(row, (8, LANES))


def index_rows(index_ref, side, block, offset):
    row = index_ref[side : side + 1, block * LANES : (block + 1) * LANES]
    return fill(row) + offset


def lookup(source, index):
    return jnp.take_along_axis(source, index, axis=1)


def residual_blocks(v_ref, s_ref, index_ref, gr, gi):
    offset = jnp.where(lax.broadcasted_iota(jnp.int32, (8, LANES), 0) >= 4, HALF, 0)
    sources = [(fill(gr[a : a + 1]), fill(gi[a : a + 1])) for a in range(2)]
    blocks = v_ref.shape[1] // LANES
    for block in range(blocks):
        lanes = pl.ds(block * LANES, LANES)
        first = index_rows(index_ref, 0, block, offset)
        second = index_rows(index_ref, 1, block, offset)
        left = [(lookup(re, first), lookup(im, first)) for re, im in sources]
        right = [(lookup(re, second), lookup(im, second)) for re, im in sources]
        for c in range(4):
            (pr, pi), (qr, qi) = left[c // 2], right[c % 2]
            cr, ci = pr * qr + pi * qi, pi * qr - pr * qi
            sr = s_ref[pl.ds(c * 8, 8), lanes]
            si = s_ref[pl.ds(32 + c * 8, 8), lanes]
            mr, mi = cmul(cr, ci, sr, si)
            yield (
                block,
                c,
                v_ref[pl.ds(c * 8, 8), lanes] - mr,
                v_ref[pl.ds(32 + c * 8, 8), lanes] - mi,
            )


def noise_into(v_ref, s_ref, index_ref, gr, gi, power_ref):
    for block, c, rr, ri in residual_blocks(v_ref, s_ref, index_ref, gr, gi):
        term = rr * rr + ri * ri
        total = term if c == 0 else total + term
        if c == 3:
            power_ref[pl.ds(block * 8, 8), :] = total


def fold_rows(ref, count, group):
    whole = group if group % 8 == 0 else math.lcm(group, 8)
    value = jnp.sum(ref[...].reshape(count * group // whole, whole, LANES), axis=0)
    if whole == group:
        return value
    total = value[0:group]
    for at in range(group, whole, group):
        total = total + value[at : at + group]
    return total


def delay_step(received_ref, delay):
    summed = fold_rows(received_ref, 64, 2)
    step = DAMPING * summed[0:1] / summed[1:2]
    low = low_half((1, LANES))
    turned = half_roll(jnp.broadcast_to(step, (8, LANES)))[0:1]
    both = jnp.concatenate([jnp.where(low, step, turned), jnp.where(low, turned, step)], axis=0)
    return delay + both


def side_by_side(left, right):
    return jnp.concatenate([left, right], axis=1)


def first_kernel(
    v_ref,
    s_ref,
    first_ref,
    second_ref,
    time_ref,
    channel_ref,
    start_ref,
    x_ref,
    power_ref,
    gain_ref,
    band_ref,
    delay_ref,
    index_ref,
    hot_ref,
):
    parts = [(part, a) for part in range(2) for a in range(2)]
    gain = jnp.concatenate(
        [side_by_side(time_ref[p, a, 0:1], time_ref[p, a, 1:2]) for p, a in parts], axis=0
    )
    band = jnp.concatenate([channel_ref[p, a] for p, a in parts], axis=0)
    band = side_by_side(band, band)
    delay = side_by_side(start_ref[...], start_ref[...])
    gain_ref[...] = gain
    band_ref[...] = band
    delay_ref[...] = delay
    baselines = first_ref.shape[1]
    padded = index_ref.shape[1]
    blocks = padded // LANES
    for block in range(blocks):
        at, end = block * LANES, min((block + 1) * LANES, baselines)
        for side, ref in enumerate((first_ref, second_ref)):
            row = ref[0:1, at:end]
            if end < at + LANES:
                row = side_by_side(row, jnp.zeros((1, at + LANES - end), jnp.int32))
            index_ref[side : side + 1, pl.ds(at, LANES)] = row
    number = lax.broadcasted_iota(jnp.int32, (HALF, LANES), 0)
    pairs = blocks // 2
    for block in range(blocks):
        at, half = block % pairs, block // pairs
        for side in range(2):
            row = index_ref[side : side + 1, pl.ds(block * LANES, LANES)]
            same = jnp.broadcast_to(row, (HALF, LANES)) == number
            rows = pl.ds((half * 2 + side) * HALF, HALF)
            hot_ref[rows, pl.ds(at * LANES, LANES)] = jnp.where(same, 1.0, 0.0).astype(
                jnp.bfloat16
            )
    _, _, (gr, gi) = chain(gain, band, delay, x_ref[0, 0])
    noise_into(v_ref, s_ref, index_ref, gr, gi, power_ref)


def next_kernel(
    v_ref, s_ref, index_ref, gain_ref, band_ref, delay_ref, received_ref, x_ref, power_ref, new_ref
):
    delay = delay_step(received_ref, delay_ref[...])
    new_ref[...] = delay
    _, _, (gr, gi) = chain(gain_ref[...], band_ref[...], delay, x_ref[0, 0])
    noise_into(v_ref, s_ref, index_ref, gr, gi, power_ref)


def last_kernel(
    v_ref, s_ref, index_ref, gain_ref, band_ref, delay_ref, received_ref, x_ref, out_ref, new_ref
):
    delay = delay_step(received_ref, delay_ref[...])
    new_ref[...] = delay
    _, _, (gr, gi) = chain(gain_ref[...], band_ref[...], delay, x_ref[0, 0])
    for block, c, rr, ri in residual_blocks(v_ref, s_ref, index_ref, gr, gi):
        lanes = pl.ds(block * LANES, LANES)
        out_ref[pl.ds(c * 8, 8), lanes] = rr
        out_ref[pl.ds(32 + c * 8, 8), lanes] = ri


def copies(value, out_ref):
    rows = value.shape[0]
    for at in range(0, out_ref.shape[0], rows):
        out_ref[pl.ds(at, rows), :] = value


def spread_kernel(parts_ref, out_ref):
    copies(jnp.sum(parts_ref[...].reshape(8, 16, LANES), axis=0), out_ref)


def weight_kernel(scale, parts_ref, out_ref):
    summed = jnp.sum(parts_ref[...].reshape(8, 16, LANES), axis=0)
    copies(1.0 / (summed * scale + EPSILON), out_ref)


def split_into(left_ref, lanes, terms):
    high = terms.astype(jnp.bfloat16)
    rest = terms - high.astype(F32)
    middle = rest.astype(jnp.bfloat16)
    low = (rest - middle.astype(F32)).astype(jnp.bfloat16)
    left_ref[0:48, lanes] = high
    left_ref[48:96, lanes] = middle
    left_ref[96:144, lanes] = low


def joined(sums):
    return sums[0:48] + (sums[48:96] + sums[96:144])


def contract(left, right):
    return lax.dot_general(left, right, (((1,), (1,)), ((), ())), preferred_element_type=F32)


def terms_of(pr, pi, qr, qi, cr, ci, power):
    rr = cr - (pr * qr + pi * qi) * power
    ri = ci - (pi * qr - pr * qi) * power
    return jnp.concatenate(
        [
            qr * rr - qi * ri,
            qr * ri + qi * rr,
            (qr * qr + qi * qi) * power,
            pr * rr + pi * ri,
            pi * rr - pr * ri,
            (pr * pr + pi * pi) * power,
        ],
        axis=0,
    )


def packed_sources(gr, gi):
    row = lax.broadcasted_iota(jnp.int32, (8, LANES), 0)
    offset = (row % 2) * HALF
    top = row < 4
    inner = (row // 2) % 2 == 0

    def pick(mask, part):
        return jnp.where(mask, fill(part[0:1]), fill(part[1:2]))

    return pick(top, gr), pick(top, gi), pick(inner, gr), pick(inner, gi), offset


def packed_lookup(sources, index_ref, block):
    p_re, p_im, q_re, q_im, offset = sources
    first = index_rows(index_ref, 0, block, offset)
    second = index_rows(index_ref, 1, block, offset)
    return lookup(p_re, first), lookup(p_im, first), lookup(q_re, second), lookup(q_im, second)


def interval_sums(stats_ref, index_ref, hot_ref, gr, gi, left_ref):
    sources = packed_sources(gr, gi)
    padded = stats_ref.shape[1]
    for block in range(padded // LANES):
        lanes = pl.ds(block * LANES, LANES)
        stats = stats_ref[0:8, lanes], stats_ref[8:16, lanes], stats_ref[16:24, lanes]
        split_into(left_ref, lanes, terms_of(*packed_lookup(sources, index_ref, block), *stats))
    middle = padded // 2
    sums = contract(left_ref[:, 0:middle], hot_ref[0:LANES, :]) + contract(
        left_ref[:, middle:padded], hot_ref[LANES : 2 * LANES, :]
    )
    sums = joined(sums)
    turned = half_roll(sums)
    low_lanes = low_half((1, LANES))
    out = []
    for kind in range(3):
        made = []
        for a in range(2):
            p, q = kind * 8 + 4 * a, 24 + kind * 8 + 2 * a

            def at(array, index):
                return array[index : index + 1]

            here = at(sums, p) + at(sums, p + 2) + (at(turned, q) + at(turned, q + 4))
            there = at(turned, p + 1) + at(turned, p + 3) + (at(sums, q + 1) + at(sums, q + 5))
            made.append(jnp.where(low_lanes, here, there))
        out.append(jnp.concatenate(made, axis=0))
    return out


def paired_sums(mix_ref, index_ref, hot_ref, hr, hi, left_ref):
    row = lax.broadcasted_iota(jnp.int32, (8, LANES), 0)
    top = row < 4
    alpha, beta = (row // 2) % 2 == 0, row % 2 == 0

    def pick(mask, part):
        return jnp.where(mask, fill(part[0:1]), fill(part[1:2]))

    p_re, p_im, q_re, q_im = pick(alpha, hr), pick(alpha, hi), pick(beta, hr), pick(beta, hi)
    pairs = mix_ref.shape[1] // LANES
    for block in range(pairs):
        lanes = pl.ds(block * LANES, LANES)
        first, second = (
            jnp.where(
                top,
                index_rows(index_ref, side, block, 0),
                index_rows(index_ref, side, block + pairs, 0),
            )
            for side in range(2)
        )
        stats = mix_ref[0:8, lanes], mix_ref[8:16, lanes], mix_ref[16:24, lanes]
        terms = terms_of(
            lookup(p_re, first),
            lookup(p_im, first),
            lookup(q_re, second),
            lookup(q_im, second),
            *stats,
        )
        split_into(left_ref, lanes, terms)
    sums = joined(contract(left_ref[...], hot_ref[...]))
    out = []
    low = low_half((2, LANES))
    for kind in range(3):

        def rows(start):
            return sums[start : start + 4, 0:LANES] + sums[start + 4 : start + 8, LANES:]

        p, q = rows(kind * 8), rows(24 + kind * 8)
        p = jnp.concatenate([p[0:1] + p[1:2], p[2:3] + p[3:4]], axis=0)
        q = q[0:2] + q[2:4]
        value = p + half_roll(q)
        out.append(jnp.where(low, value, half_roll(value)))
    return out


def time_kernel(
    v_ref,
    s_ref,
    weight_ref,
    index_ref,
    hot_ref,
    gain_ref,
    band_ref,
    delay_ref,
    x_ref,
    stats_ref,
    send_ref,
    kept_ref,
    real_ref,
    imag_ref,
    power_ref,
    left_ref,
):
    blocks = v_ref.shape[1] // LANES
    baselines = kept_ref.shape[1]
    for block in range(blocks):
        lanes = pl.ds(block * LANES, LANES)
        weight = weight_ref[pl.ds(block * 8, 8), :]
        width = min(LANES, baselines - block * LANES)
        kept_ref[:, pl.ds(block * LANES, width)] = weight[:, 0:width]
        for c in range(4):
            sr, si = s_ref[pl.ds(c * 8, 8), lanes], s_ref[pl.ds(32 + c * 8, 8), lanes]
            vr, vi = v_ref[pl.ds(c * 8, 8), lanes], v_ref[pl.ds(32 + c * 8, 8), lanes]
            xr, xi = conj_mul(sr, si, vr, vi)
            rows = pl.ds(block * 32 + c * 8, 8)
            real_ref[rows, :] = weight * xr
            imag_ref[rows, :] = weight * xi
            power_ref[rows, :] = weight * (sr * sr + si * si)
        for slot, ref in enumerate((real_ref, imag_ref, power_ref)):
            parts = [ref[pl.ds(block * 32 + t, 8, stride=4), :] for t in range(4)]
            stats_ref[slot * 8 : slot * 8 + 8, lanes] = parts[0] + parts[1] + (parts[2] + parts[3])
    _, (hr, hi), (gr, gi) = chain(gain_ref[...], band_ref[...], delay_ref[...], x_ref[0, 0])
    ur, ui, w = interval_sums(stats_ref, index_ref, hot_ref, gr, gi, left_ref)
    nr, ni = conj_mul(hr, hi, ur, ui)
    packed = jnp.concatenate([nr, ni, (hr * hr + hi * hi) * w], axis=0)
    repeated = jnp.concatenate([packed] * 4, axis=0)
    for at in range(16):
        send_ref[pl.ds(at * 24, 24), :] = repeated


def stepped(numerator_re, numerator_im, denominator):
    return jnp.concatenate(
        [DAMPING * numerator_re / denominator, DAMPING * numerator_im / denominator], axis=0
    )


def mix_kernel(
    stats_ref, received_ref, index_ref, gain_ref, new_ref, mix_ref, real_ref, imag_ref, power_ref
):
    summed = fold_rows(received_ref, 64, 6)
    gain = gain_ref[...] + stepped(summed[0:2], summed[2:4], summed[4:6])
    new_ref[...] = gain
    sources = packed_sources(gain[0:2], gain[2:4])
    blocks = stats_ref.shape[1] // LANES
    pairs = blocks // 2
    for block in range(blocks):
        lanes = pl.ds(block * LANES, LANES)
        pr, pi, qr, qi = packed_lookup(sources, index_ref, block)
        er, ei = conj_mul(pr, pi, qr, qi)
        ar, ai = cmul(er, ei, stats_ref[0:8, lanes], stats_ref[8:16, lanes])
        rows = pl.ds((block % pairs) * 16 + (block // pairs) * 8, 8)
        real_ref[rows, :] = ar
        imag_ref[rows, :] = ai
        power_ref[rows, :] = (pr * pr + pi * pi) * ((qr * qr + qi * qi) * stats_ref[16:24, lanes])
    for pair in range(pairs):
        lanes = pl.ds(pair * LANES, LANES)
        for slot, ref in enumerate((real_ref, imag_ref, power_ref)):
            mix_ref[slot * 8 : slot * 8 + 8, lanes] = (
                ref[pl.ds(pair * 16, 8, stride=2), :] + ref[pl.ds(pair * 16 + 1, 8, stride=2), :]
            )


def solve_kernel(
    mix_ref, index_ref, hot_ref, band_ref, delay_ref, x_ref, new_ref, send_ref, left_ref
):
    x = x_ref[0, 0]
    angle = TURN * delay_ref[...] * x
    kr, ki = jnp.cos(angle), jnp.sin(angle)
    band = band_ref[...]
    hr, hi = cmul(band[0:2], band[2:4], kr, ki)
    ur, ui, w = paired_sums(mix_ref, index_ref, hot_ref, hr, hi, left_ref)
    nr, ni = conj_mul(kr, ki, ur, ui)
    band = band + stepped(nr, ni, (kr * kr + ki * ki) * w)
    new_ref[...] = band
    hr, hi = cmul(band[0:2], band[2:4], kr, ki)
    ur, ui, w = paired_sums(mix_ref, index_ref, hot_ref, hr, hi, left_ref)
    turning = TURN * x
    n = turning * (hr * ui - hi * ur)
    d = (turning * turning) * ((hr * hr + hi * hi) * w)
    low = low_half((1, LANES))
    pair = jnp.concatenate(
        [jnp.where(low, n[0:1], n[1:2]), jnp.where(low, d[0:1], d[1:2])], axis=0
    )
    copies(jnp.concatenate([pair] * 4, axis=0), send_ref)


def call(body, outs, operands, scratch=()):
    vmem = pl.BlockSpec(memory_space=pltpu.VMEM)
    smem = pl.BlockSpec(memory_space=pltpu.SMEM)
    return pl.pallas_call(
        body,
        out_shape=tuple(
            o if isinstance(o, jax.ShapeDtypeStruct) else jax.ShapeDtypeStruct(o, F32)
            for o in outs
        ),
        in_specs=[smem if o.shape == (1, 1) else vmem for o in operands],
        out_specs=tuple(vmem for _ in outs),
        scratch_shapes=list(scratch),
        compiler_params=pltpu.CompilerParams(vmem_limit_bytes=12 << 20),
    )(*operands)


def exchange(array, axis):
    devices = lax.axis_size(axis)
    chunks = array.reshape(devices, 1, -1)
    return lax.all_to_all(chunks, axis, 0, 0, tiled=True).reshape(array.shape)


def pair_total(array):
    for axis in ("tm_1", "tm_0"):
        array = array + lax.ppermute(array, axis, [(0, 1), (1, 0)])
    return array


def shards(
    visibilities, sky_model, gain_time, gain_band, delay_start, first_antenna, second_antenna
):
    antennas = gain_time.shape[-1]
    baselines = visibilities.shape[4]
    padded = -(-baselines // (2 * LANES)) * 2 * LANES
    blocks = padded // LANES
    times = visibilities.shape[2]
    channels = lax.axis_size(FREQ)
    x = (lax.axis_index(FREQ).astype(F32) + 0.5) / channels - 0.5
    x = x.reshape(1, 1)

    def plane(array):
        flat = array.reshape(-1, baselines)
        return jnp.pad(flat, ((0, 0), (0, padded - baselines)))

    v, s = plane(visibilities), plane(sky_model)
    square = (blocks * 8, LANES)
    left = pltpu.VMEM((144, padded), jnp.bfloat16)
    half_left = pltpu.VMEM((144, padded // 2), jnp.bfloat16)
    tall = pltpu.VMEM((blocks * 32, LANES), F32)
    short = pltpu.VMEM(square, F32)
    power, gain, band, delay, index, hot = call(
        first_kernel,
        [
            square,
            (4, LANES),
            (4, LANES),
            (2, LANES),
            jax.ShapeDtypeStruct((8, padded), jnp.int32),
            jax.ShapeDtypeStruct((4 * HALF, padded // 2), jnp.bfloat16),
        ],
        (
            v,
            s,
            first_antenna.reshape(1, -1),
            second_antenna.reshape(1, -1),
            gain_time,
            gain_band,
            delay_start,
            x,
        ),
    )
    for sweep in range(SWEEPS):
        if sweep > 0:
            power, delay = call(
                next_kernel, [square, delay.shape], (v, s, index, gain, band, delay, received, x)
            )
        (shared,) = call(spread_kernel, [square], (exchange(power, Z),))
        (mine,) = call(
            functools.partial(weight_kernel, 1.0 / (4 * channels)),
            [square],
            (exchange(shared, YX),),
        )
        weight = exchange(mine, Z)
        outs, scratch = [(24, padded), (384, LANES)], [tall, tall, tall, left]
        if sweep < SWEEPS - 1:
            scratch = [pltpu.VMEM((times, baselines), F32)] + scratch
        else:
            outs = outs + [(times, baselines)]
        stats, send, *kept = call(
            time_kernel, outs, (v, s, weight, index, hot, gain, band, delay, x), scratch
        )
        gain, mix = call(
            mix_kernel,
            [gain.shape, (24, padded // 2)],
            (stats, exchange(send, FREQ), index, gain),
            (short, short, short),
        )
        band, send = call(
            solve_kernel,
            [band.shape, (128, LANES)],
            (pair_total(mix), index, hot, band, delay, x),
            (half_left,),
        )
        received = exchange(send, FREQ)
    residual, delay = call(
        last_kernel, [v.shape, delay.shape], (v, s, index, gain, band, delay, received, x)
    )
    return (
        gain.reshape(gain_time.shape),
        band[:, :antennas].reshape(gain_band.shape),
        delay[:, :antennas],
        kept[0],
        residual[:, :baselines].reshape(visibilities.shape),
    )


def solution(mesh):
    split = Mesh(
        mesh.devices.reshape(2, 2, 4, 2, 8), ("tm_0", "tm_1", "freq_0", "freq_1", "freq_2")
    )
    placed = (
        P(None, None, TM, FREQ, None),
        P(None, None, TM, FREQ, None),
        P(None, None, TM, None),
        P(None, None, FREQ, None),
        P(),
        P(),
        P(),
    )
    return jax.shard_map(
        shards,
        mesh=split,
        in_specs=placed,
        out_specs=(
            P(None, None, TM, None),
            P(None, None, FREQ, None),
            P(),
            P(TM, None),
            P(None, None, TM, FREQ, None),
        ),
        check_vma=False,
    )
```

time: 175 us -> 165 us (0.943)
  blocking collectives: 82.1 us -> 123 us
  waiting for transfers between devices: 47.5 us -> 20.9 us
  starting transfers between devices: 28.8 us -> 7.84 us
  local copies, waits for them, and re-layouts: 6.78 us -> 4.21 us
    all_to_all x5 -> x9, blocking collectives: 82.1 us -> 123 us  [exchange(): return lax.all_to_all(chunks, axis, 0, 0, tiled=True).reshape(array.shape)]
    all_to_all x3 -> x1, waiting for transfers between devices: 34.2 us -> 11.5 us  [exchange(): return lax.all_to_all(chunks, axis, 0, 0, tiled=True).reshape(array.shape)]
    all_to_all x3 -> x1, starting transfers between devices: 22.9 us -> 4.62 us  [exchange(): return lax.all_to_all(chunks, axis, 0, 0, tiled=True).reshape(array.shape)]
    ppermute x8 -> x4, waiting for transfers between devices: 13.3 us -> 9.42 us  [pair_total(): array = array + lax.ppermute(array, axis, [(0, 1), (1, 0)])]
    ppermute x8 -> x4, starting transfers between devices: 5.87 us -> 3.22 us  [pair_total(): array = array + lax.ppermute(array, axis, [(0, 1), (1, 0)])]
    unnamed x18 -> x17, local copies, waits for them, and re-layouts: 5.28 us -> 3.46 us
    pallas_call x11 -> x13, Pallas kernels: 7.07 us -> 7.29 us  [call(): pl.pallas_call(body, out_shape=tuple((o if isinstance(o, jax.ShapeDtypeSt...]
  transfers between devices with their start and end apart: 11 -> 5, of which waited for: 11 -> 5; matrix products, arithmetic and copies ran while one was open for 1% -> 0% of each run, Pallas kernels for 0% -> 0%
where the time goes in v1:
time: 165 us; the launch traced here: 164 us
  blocking collectives  123 us (75%)
  waiting for transfers between devices  20.9 us (13%)
  starting transfers between devices  7.84 us (5%)
  Pallas kernels  7.29 us (4%)
  local copies, waits for them, and re-layouts  4.21 us (3%)
    all_to_all x9, blocking collectives, exchange(): return lax.all_to_all(chunks, axis, 0, 0, tiled=True).reshape(array.shape)  123 us
    all_to_all x1, waiting for transfers between devices, exchange(): return lax.all_to_all(chunks, axis, 0, 0, tiled=True).reshape(array.shape)  11.5 us
    ppermute x4, waiting for transfers between devices, pair_total(): array = array + lax.ppermute(array, axis, [(0, 1), (1, 0)])  9.42 us
    pallas_call x13, Pallas kernels, call(): pl.pallas_call(body, out_shape=tuple((o if isinstance(o, jax.ShapeDtypeSt...  7.29 us
    all_to_all x1, starting transfers between devices, exchange(): return lax.all_to_all(chunks, axis, 0, 0, tiled=True).reshape(array.shape)  4.62 us
    unnamed x17, local copies, waits for them, and re-layouts  3.46 us
  transfers between devices with their start and end apart: 5, of which 5 were waited for; matrix products, arithmetic and copies ran while one was open for 0% of the time, Pallas kernels for 0%

profile of v1, /device:TPU:2, one launch (start us, length us, event | category | flops | bytes accessed | tf_op | source)
XLA Modules:
  0.0 164.4 jit_solution(10848379474764602065)
XLA Ops:
  0.6 1.3 copy.26
  3.4 16.6 %all_to_all.50 = f32[8,1,2048]{2,1,0:T(1,128)S(1)} all-to-all(f32[8,1,2048]{2,1,0:T(1,128)S(1)} %bitcast.49), channel_id=1, replica_groups=mesh['tm_0'=2,'tm_1'=2,'freq_0'=4,'freq_1'=2,'freq_2'=8] {'freq_2'}, dimensions={0} | all-to-all | bytes 131072 | tf_op jit(solution)/shard_map/all_to_all | solution.py:453
  20.1 13.7 %all_to_all.51 = f32[8,1,2048]{2,1,0:T(1,128)S(1)} all-to-all(f32[8,1,2048]{2,1,0:T(1,128)S(1)} %bitcast.40), channel_id=1, replica_groups=mesh['tm_0'=2,'tm_1'=2,'freq_0'=4,'freq_1'=2,'freq_2'=8] {'freq_0','freq..., dimensions={0} | all-to-all | bytes 131072 | tf_op jit(solution)/shard_map/all_to_all | solution.py:453
  33.8 10.8 %all_to_all.52 = f32[8,1,2048]{2,1,0:T(1,128)S(1)} all-to-all(f32[8,1,2048]{2,1,0:T(1,128)S(1)} %bitcast.42), channel_id=1, replica_groups=mesh['tm_0'=2,'tm_1'=2,'freq_0'=4,'freq_1'=2,'freq_2'=8] {'freq_2'}, dimensions={0} | all-to-all | bytes 131072 | tf_op jit(solution)/shard_map/all_to_all | solution.py:453
  44.5 0.8 shard_map.113
  45.3 16.9 %all_to_all.53 = f32[64,1,768]{2,1,0:T(1,128)S(1)} all-to-all(f32[64,1,768]{2,1,0:T(1,128)S(1)} %bitcast.48), channel_id=1, replica_groups=mesh['tm_0'=2,'tm_1'=2,'freq_0'=4,'freq_1'=2,'freq_2'=8] {'freq_0','freq..., dimensions={0} | all-to-all | bytes 393216 | tf_op jit(solution)/shard_map/all_to_all | solution.py:453
  62.6 1.3 collective-permute-done
  63.9 1.5 collective-permute-start.1
  65.4 3.4 %collective-permute-done.1 = f32[24,1024]{1,0:T(8,128)S(1)} collective-permute-done((f32[24,1024]{1,0:T(8,128)S(1)}, f32[24,1024]{1,0:T(8,128)S(1)}, u32[]{:S(2)}, u32[]{:S(2)}) %collective-permute-start.1) | collective-permute-done | bytes 98336 | tf_op jit(solution)/shard_map/ppermute | solution.py:458
  68.9 1.3 shard_map.115
  70.2 16.4 %all_to_all.54 = f32[64,1,256]{2,1,0:T(1,128)S(1)} all-to-all(f32[64,1,256]{2,1,0:T(1,128)S(1)} %bitcast.50), channel_id=1, replica_groups=mesh['tm_0'=2,'tm_1'=2,'freq_0'=4,'freq_1'=2,'freq_2'=8] {'freq_0','freq..., dimensions={0} | all-to-all | bytes 131072 | tf_op jit(solution)/shard_map/all_to_all | solution.py:453
  87.0 10.8 %all_to_all.55 = f32[8,1,2048]{2,1,0:T(1,128)S(1)} all-to-all(f32[8,1,2048]{2,1,0:T(1,128)S(1)} %bitcast.51), channel_id=1, replica_groups=mesh['tm_0'=2,'tm_1'=2,'freq_0'=4,'freq_1'=2,'freq_2'=8] {'freq_2'}, dimensions={0} | all-to-all | bytes 131072 | tf_op jit(solution)/shard_map/all_to_all | solution.py:453
  97.8 10.5 %all_to_all.56 = f32[8,1,2048]{2,1,0:T(1,128)S(1)} all-to-all(f32[8,1,2048]{2,1,0:T(1,128)S(1)} %bitcast.44), channel_id=1, replica_groups=mesh['tm_0'=2,'tm_1'=2,'freq_0'=4,'freq_1'=2,'freq_2'=8] {'freq_0','freq..., dimensions={0} | all-to-all | bytes 131072 | tf_op jit(solution)/shard_map/all_to_all | solution.py:453
  108.3 10.8 %all_to_all.57 = f32[8,1,2048]{2,1,0:T(1,128)S(1)} all-to-all(f32[8,1,2048]{2,1,0:T(1,128)S(1)} %bitcast.46), channel_id=1, replica_groups=mesh['tm_0'=2,'tm_1'=2,'freq_0'=4,'freq_1'=2,'freq_2'=8] {'freq_2'}, dimensions={0} | all-to-all | bytes 131072 | tf_op jit(solution)/shard_map/all_to_all | solution.py:453
  119.1 1.1 shard_map.119
  120.2 16.9 %all_to_all.58 = f32[64,1,768]{2,1,0:T(1,128)S(1)} all-to-all(f32[64,1,768]{2,1,0:T(1,128)S(1)} %bitcast.47), channel_id=1, replica_groups=mesh['tm_0'=2,'tm_1'=2,'freq_0'=4,'freq_1'=2,'freq_2'=8] {'freq_0','freq..., dimensions={0} | all-to-all | bytes 393216 | tf_op jit(solution)/shard_map/all_to_all | solution.py:453
  137.5 1.3 collective-permute-done.2
  138.8 1.5 collective-permute-start.3
  140.3 3.4 %collective-permute-done.3 = f32[24,1024]{1,0:T(8,128)S(1)} collective-permute-done((f32[24,1024]{1,0:T(8,128)S(1)}, f32[24,1024]{1,0:T(8,128)S(1)}, u32[]{:S(2)}, u32[]{:S(2)}) %collective-permute-start.3) | collective-permute-done | bytes 98336 | tf_op jit(solution)/shard_map/ppermute | solution.py:458
  143.7 1.9 %shard_map.121 = (f32[4,128]{1,0:T(4,128)}, f32[128,128]{1,0:T(8,128)}) custom-call(f32[24,1024]{1,0:T(8,128)S(1)} %add.32.mix_ref, s32[8,2048]{1,0:T(8,128)S(1)} %get-tuple-element.28.index_ref, bf16[256,1024]{1,0:T(8,128)(2,1)S(1)} %get-tuple-element.30.hot_ref, f32[4,128]{1,0:T(4,128)S(1)} %get-tuple-element.38.band_ref, ...), custom_call_target="tpu_custom_call" | custom-call | tf_op jit(solution)/shard_map/pallas_call | solution.py:437
  145.7 4.6 %all-to-all-start.9 = ((f32[64,1,256]{2,1,0:T(1,128)}), f32[64,1,256]{2,1,0:T(1,128)S(1)}, u32[]{:S(2)}, u32[]{:S(2)}) async-start(f32[64,1,256]{2,1,0:T(1,128)} %bitcast.23), calls=%async_computation.9 | async-start | bytes 131072 | tf_op jit(solution)/shard_map/all_to_all | solution.py:453
  150.3 0.7 reshape.117
  151.0 11.5 %all-to-all-done.9 = f32[64,1,256]{2,1,0:T(1,128)S(1)} async-done(((f32[64,1,256]{2,1,0:T(1,128)}), f32[64,1,256]{2,1,0:T(1,128)S(1)}, u32[]{:S(2)}, u32[]{:S(2)}) %all-to-all-start.9) | async-done | bytes 65568 | tf_op jit(solution)/shard_map/all_to_all | solution.py:453
  163.1 1.3 copy.25
  (32 shorter events, 3.4 us)
Async XLA Ops:
  0.6 1.3 copy-start.6
  2.1 0.7 copy-start.1
  2.1 0.7 copy-start.2
  2.2 0.7 copy-start
  2.2 0.7 copy-start.3
  2.2 0.7 copy-start.5
  62.5 1.4 collective-permute-start
  63.9 4.9 %collective-permute-start.1 = (f32[24,1024]{1,0:T(8,128)S(1)}, f32[24,1024]{1,0:T(8,128)S(1)}, u32[]{:S(2)}, u32[]{:S(2)}) collective-permute-start(f32[24,1024]{1,0:T(8,128)S(1)} %add.29), channel_id=1, source_target_pairs={{0,128},{128,0},{1,129},{129,1},{2,130},{130,2},{3,131},{131,3},{4... | collective-permute-start | bytes 294920 | tf_op jit(solution)/shard_map/ppermute | solution.py:458
  137.4 1.4 collective-permute-start.2
  138.8 4.9 %collective-permute-start.3 = (f32[24,1024]{1,0:T(8,128)S(1)}, f32[24,1024]{1,0:T(8,128)S(1)}, u32[]{:S(2)}, u32[]{:S(2)}) collective-permute-start(f32[24,1024]{1,0:T(8,128)S(1)} %add.31), channel_id=1, source_target_pairs={{0,128},{128,0},{1,129},{129,1},{2,130},{130,2},{3,131},{131,3},{4... | collective-permute-start | bytes 294920 | tf_op jit(solution)/shard_map/ppermute | solution.py:458
  145.7 16.8 %all-to-all-start.9 = ((f32[64,1,256]{2,1,0:T(1,128)}), f32[64,1,256]{2,1,0:T(1,128)S(1)}, u32[]{:S(2)}, u32[]{:S(2)}) async-start(f32[64,1,256]{2,1,0:T(1,128)} %bitcast.23), calls=%async_computation.9 | async-start | bytes 131072 | tf_op jit(solution)/shard_map/all_to_all | solution.py:453
  151.0 11.5 %copy-start.4 = (f32[4,128]{1,0:T(4,128)S(1)}, f32[4,128]{1,0:T(4,128)}, u32[]{:S(2)}) copy-start(f32[4,128]{1,0:T(4,128)} %get-tuple-element.46.band_ref) | copy-start | bytes 6148

commit v2 on v1

v2 whole, which is shorter than its diff:
```python
import functools
import math

import jax
import jax.numpy as jnp
from jax import lax
from jax.experimental import pallas as pl
from jax.experimental.pallas import tpu as pltpu
from jax.sharding import Mesh
from jax.sharding import PartitionSpec as P

SWEEPS = 2
TURN = 2.0 * math.pi
DAMPING = 0.5
EPSILON = 1e-06
LANES = 128
HALF = 64
PLANES = 64
CHUNK = 4 * PLANES + 8
FREQ = ("freq_0", "freq_1", "freq_2")
TM = ("tm_0", "tm_1")
YX = ("freq_0", "freq_1")
Z = "freq_2"
F32 = jnp.float32


def half_roll(array):
    return pltpu.roll(array, HALF, 1)


def low_half(shape):
    return lax.broadcasted_iota(jnp.int32, shape, 1) < HALF


def cmul(ar, ai, br, bi):
    return ar * br - ai * bi, ar * bi + ai * br


def conj_mul(ar, ai, br, bi):
    return ar * br + ai * bi, ar * bi - ai * br


def chain(gain, band, delay, x):
    angle = TURN * delay * x
    kr, ki = jnp.cos(angle), jnp.sin(angle)
    hr, hi = cmul(band[0:2], band[2:4], kr, ki)
    gr, gi = cmul(gain[0:2], gain[2:4], hr, hi)
    return (kr, ki), (hr, hi), (gr, gi)


def fill(row):
    return jnp.broadcast_to(row, (8, LANES))


def index_rows(index_ref, side, block, offset):
    return fill(index_ref[block * 8 + side : block * 8 + side + 1, :]) + offset


def lookup(source, index):
    return jnp.take_along_axis(source, index, axis=1)


def cell_base(chunk, inner):
    return chunk * CHUNK + inner * PLANES


def parts_of(data_ref, base, c):
    return tuple(
        data_ref[pl.ds(base + kind * 2 * PLANES + part * 32 + c * 8, 8), :]
        for kind in range(2)
        for part in range(2)
    )


def residual_of(data_ref, base, left, right):
    for c in range(4):
        (pr, pi), (qr, qi) = left[c // 2], right[c % 2]
        cr, ci = pr * qr + pi * qi, pi * qr - pr * qi
        vr, vi, sr, si = parts_of(data_ref, base, c)
        mr, mi = cmul(cr, ci, sr, si)
        yield c, vr - mr, vi - mi


def time_offset():
    return jnp.where(lax.broadcasted_iota(jnp.int32, (8, LANES), 0) >= 4, HALF, 0)


def stacked(pair):
    return jnp.concatenate([fill(pair[0:1]), fill(pair[1:2])], axis=0)


def band_chain(bands, delay, x0, step):
    row = lax.broadcasted_iota(jnp.int32, (16, LANES), 0) % 8
    x = x0 + step * row.astype(F32)
    angle = TURN * stacked(delay) * x
    return cmul(bands[0:16], bands[16:32], jnp.cos(angle), jnp.sin(angle))


def noise_into(data_ref, mine_ref, gain, bands, delay, x0, step, power_ref):
    hr, hi = band_chain(bands, delay, x0, step)
    gr, gi = cmul(stacked(gain[0:2]), stacked(gain[2:4]), hr, hi)
    offset = time_offset()
    index = [[index_rows(mine_ref, side, inner, offset) for side in range(2)] for inner in range(2)]
    totals = [None, None]
    for k in range(8):
        sources = [
            (fill(gr[a * 8 + k : a * 8 + k + 1]), fill(gi[a * 8 + k : a * 8 + k + 1]))
            for a in range(2)
        ]
        for inner in range(2):
            left, right = (
                [(lookup(re, at), lookup(im, at)) for re, im in sources] for at in index[inner]
            )
            for _, rr, ri in residual_of(data_ref, cell_base(k, inner), left, right):
                term = rr * rr + ri * ri
                totals[inner] = term if totals[inner] is None else totals[inner] + term
    copies(jnp.concatenate(totals, axis=0), power_ref)


def delay_step(received_ref, delay):
    summed = jnp.sum(received_ref[...].reshape(32, 8, LANES), axis=0)
    summed = summed[0:4] + summed[4:8]
    step = DAMPING * summed[0:1] / summed[1:2]
    low = low_half((1, LANES))
    turned = half_roll(jnp.broadcast_to(step, (8, LANES)))[0:1]
    both = jnp.concatenate([jnp.where(low, step, turned), jnp.where(low, turned, step)], axis=0)
    return delay + both


def side_by_side(left, right):
    return jnp.concatenate([left, right], axis=1)


def arrange_kernel(v_ref, s_ref, channel_ref, data_ref):
    baselines = v_ref.shape[1]
    band = own_band(channel_ref)
    for chunk in range(8):
        for inner in range(2):
            at = (2 * chunk + inner) * LANES
            end = min(at + LANES, baselines)
            for kind, ref in enumerate((v_ref, s_ref)):
                value = ref[:, at:end]
                if end < at + LANES:
                    value = side_by_side(value, jnp.zeros((PLANES, at + LANES - end), F32))
                data_ref[pl.ds(cell_base(chunk, inner) + kind * 2 * PLANES, PLANES), :] = value
        data_ref[pl.ds(chunk * CHUNK + 4 * PLANES, 8), :] = jnp.concatenate([band, band], axis=0)


def own_band(channel_ref):
    parts = [(part, a) for part in range(2) for a in range(2)]
    band = jnp.concatenate([channel_ref[p, a] for p, a in parts], axis=0)
    return side_by_side(band, band)


def table_kernel(
    first_ref,
    second_ref,
    time_ref,
    channel_ref,
    start_ref,
    member_ref,
    gain_ref,
    band_ref,
    delay_ref,
    index_ref,
    hot_ref,
    mine_ref,
    mine_hot_ref,
):
    parts = [(part, a) for part in range(2) for a in range(2)]
    gain_ref[...] = jnp.concatenate(
        [side_by_side(time_ref[p, a, 0:1], time_ref[p, a, 1:2]) for p, a in parts], axis=0
    )
    band_ref[...] = own_band(channel_ref)
    delay_ref[...] = side_by_side(start_ref[...], start_ref[...])
    baselines = first_ref.shape[1]
    blocks = index_ref.shape[0] // 8
    for block in range(blocks):
        at, end = block * LANES, min((block + 1) * LANES, baselines)
        rows = []
        for ref in (first_ref, second_ref):
            row = ref[0:1, at:end]
            if end < at + LANES:
                row = side_by_side(row, jnp.zeros((1, at + LANES - end), jnp.int32))
            rows.append(row)
        index_ref[pl.ds(block * 8, 8), :] = jnp.concatenate(rows * 4, axis=0)
    number = lax.broadcasted_iota(jnp.int32, (HALF, LANES), 0)

    def marks(ref, block, side):
        row = ref[block * 8 + side : block * 8 + side + 1, :]
        same = jnp.broadcast_to(row, (HALF, LANES)) == number
        return jnp.where(same, 1.0, 0.0).astype(jnp.bfloat16)

    pairs = blocks // 2
    for block in range(blocks):
        at, half = block % pairs, block // pairs
        for side in range(2):
            rows = pl.ds((half * 2 + side) * HALF, HALF)
            hot_ref[rows, pl.ds(at * LANES, LANES)] = marks(index_ref, block, side)
    mine_ref[...] = index_ref[pl.ds(pl.multiple_of(member_ref[0, 0] * 16, 16), 16), :]
    for inner in range(2):
        for side in range(2):
            mine_hot_ref[pl.ds(side * HALF, HALF), pl.ds(inner * LANES, LANES)] = marks(
                mine_ref, inner, side
            )


def first_kernel(
    step, data_ref, mine_ref, gain_ref, delay_ref, x_ref, power_ref, bands_ref
):
    at = [k * CHUNK + 4 * PLANES for k in range(8)]
    bands = jnp.concatenate(
        [data_ref[at[k] + r : at[k] + r + 1, :] for r in range(4) for k in range(8)], axis=0
    )
    bands_ref[...] = bands
    noise_into(
        data_ref, mine_ref, gain_ref[...], bands, delay_ref[...], x_ref[0, 0], step, power_ref
    )


def next_kernel(
    step,
    data_ref,
    mine_ref,
    gain_ref,
    delay_ref,
    received_ref,
    z_ref,
    x_ref,
    power_ref,
    bands_ref,
    new_ref,
):
    delay = delay_step(received_ref, delay_ref[...])
    new_ref[...] = delay
    z = z_ref[0, 0]
    re, im = [], []
    odd = z % 2 == 1
    for k in range(8):
        value = jnp.zeros((8, LANES), F32)
        for j in range(4):
            found = received_ref[pl.ds(k * 32 + j * 8, 8), :]
            value = jnp.where(z // 2 == j, found, value)
        value = jnp.where(odd, value[4:8], value[0:4])
        re.append(value[2:3])
        im.append(value[3:4])
    low = low_half((8, LANES))
    bands = []
    for rows in (re, im):
        value = jnp.concatenate(rows, axis=0)
        turned = half_roll(value)
        bands += [jnp.where(low, value, turned), jnp.where(low, turned, value)]
    bands = jnp.concatenate(bands, axis=0)
    bands_ref[...] = bands
    noise_into(data_ref, mine_ref, gain_ref[...], bands, delay, x_ref[0, 0], step, power_ref)


def last_kernel(
    data_ref, index_ref, gain_ref, band_ref, delay_ref, received_ref, x_ref, out_ref, new_ref
):
    delay = delay_step(received_ref, delay_ref[...])
    new_ref[...] = delay
    _, _, (gr, gi) = chain(gain_ref[...], band_ref[...], delay, x_ref[0, 0])
    offset = time_offset()
    sources = [(fill(gr[a : a + 1]), fill(gi[a : a + 1])) for a in range(2)]
    for block in range(index_ref.shape[0] // 8):
        left, right = (
            [(lookup(re, at), lookup(im, at)) for re, im in sources]
            for at in (index_rows(index_ref, side, block, offset) for side in range(2))
        )
        lanes = pl.ds(block * LANES, LANES)
        base = cell_base(block // 2, block % 2)
        for c, rr, ri in residual_of(data_ref, base, left, right):
            out_ref[pl.ds(c * 8, 8), lanes] = rr
            out_ref[pl.ds(32 + c * 8, 8), lanes] = ri


def copies(value, out_ref):
    rows = value.shape[0]
    for at in range(0, out_ref.shape[0], rows):
        out_ref[pl.ds(at, rows), :] = value


def split_into(left_ref, lanes, terms):
    high = terms.astype(jnp.bfloat16)
    rest = terms - high.astype(F32)
    middle = rest.astype(jnp.bfloat16)
    low = (rest - middle.astype(F32)).astype(jnp.bfloat16)
    left_ref[0:48, lanes] = high
    left_ref[48:96, lanes] = middle
    left_ref[96:144, lanes] = low


def joined(sums):
    return sums[0:48] + (sums[48:96] + sums[96:144])


def contract(left, right):
    return lax.dot_general(left, right, (((1,), (1,)), ((), ())), preferred_element_type=F32)


def terms_of(pr, pi, qr, qi, cr, ci, power):
    rr = cr - (pr * qr + pi * qi) * power
    ri = ci - (pi * qr - pr * qi) * power
    return jnp.concatenate(
        [
            qr * rr - qi * ri,
            qr * ri + qi * rr,
            (qr * qr + qi * qi) * power,
            pr * rr + pi * ri,
            pi * rr - pr * ri,
            (pr * pr + pi * pi) * power,
        ],
        axis=0,
    )


def packed_sources(gr, gi):
    row = lax.broadcasted_iota(jnp.int32, (8, LANES), 0)
    offset = (row % 2) * HALF
    top = row < 4
    inner = (row // 2) % 2 == 0

    def pick(mask, part):
        return jnp.where(mask, fill(part[0:1]), fill(part[1:2]))

    return pick(top, gr), pick(top, gi), pick(inner, gr), pick(inner, gi), offset


def packed_lookup(sources, index_ref, block):
    p_re, p_im, q_re, q_im, offset = sources
    first = index_rows(index_ref, 0, block, offset)
    second = index_rows(index_ref, 1, block, offset)
    return lookup(p_re, first), lookup(p_im, first), lookup(q_re, second), lookup(q_im, second)


def packed_stats(data_ref, base, weight, scratch):
    for c in range(4):
        vr, vi, sr, si = parts_of(data_ref, base, c)
        xr, xi = conj_mul(sr, si, vr, vi)
        for ref, value in zip(scratch, (xr, xi, sr * sr + si * si)):
            ref[pl.ds(c * 8, 8), :] = weight * value
    out = []
    for ref in scratch:
        parts = [ref[pl.ds(t, 8, stride=4), :] for t in range(4)]
        out.append(parts[0] + parts[1] + (parts[2] + parts[3]))
    return out


def antenna_rows(sums):
    turned = half_roll(sums)
    low_lanes = low_half((1, LANES))
    out = []
    for kind in range(3):
        made = []
        for a in range(2):
            p, q = kind * 8 + 4 * a, 24 + kind * 8 + 2 * a

            def at(array, index):
                return array[index : index + 1]

            here = at(sums, p) + at(sums, p + 2) + (at(turned, q) + at(turned, q + 4))
            there = at(turned, p + 1) + at(turned, p + 3) + (at(sums, q + 1) + at(sums, q + 5))
            made.append(jnp.where(low_lanes, here, there))
        out.append(jnp.concatenate(made, axis=0))
    return out


def paired_sums(mix_ref, index_ref, hot_ref, hr, hi, left_ref):
    row = lax.broadcasted_iota(jnp.int32, (8, LANES), 0)
    top = row < 4
    alpha, beta = (row // 2) % 2 == 0, row % 2 == 0

    def pick(mask, part):
        return jnp.where(mask, fill(part[0:1]), fill(part[1:2]))

    p_re, p_im, q_re, q_im = pick(alpha, hr), pick(alpha, hi), pick(beta, hr), pick(beta, hi)
    pairs = mix_ref.shape[1] // LANES
    for block in range(pairs):
        lanes = pl.ds(block * LANES, LANES)
        first, second = (
            jnp.where(
                top,
                index_rows(index_ref, side, block, 0),
                index_rows(index_ref, side, block + pairs, 0),
            )
            for side in range(2)
        )
        stats = mix_ref[0:8, lanes], mix_ref[8:16, lanes], mix_ref[16:24, lanes]
        terms = terms_of(
            lookup(p_re, first),
            lookup(p_im, first),
            lookup(q_re, second),
            lookup(q_im, second),
            *stats,
        )
        split_into(left_ref, lanes, terms)
    sums = joined(contract(left_ref[...], hot_ref[...]))
    out = []
    low = low_half((2, LANES))
    for kind in range(3):

        def rows(start):
            return sums[start : start + 4, 0:LANES] + sums[start + 4 : start + 8, LANES:]

        p, q = rows(kind * 8), rows(24 + kind * 8)
        p = jnp.concatenate([p[0:1] + p[1:2], p[2:3] + p[3:4]], axis=0)
        q = q[0:2] + q[2:4]
        value = p + half_roll(q)
        out.append(jnp.where(low, value, half_roll(value)))
    return out


def time_kernel(
    scale,
    step,
    data_ref,
    parts_ref,
    mine_ref,
    hot_ref,
    gain_ref,
    bands_ref,
    delay_ref,
    z_ref,
    x_ref,
    send_ref,
    left_ref,
    *scratch,
):
    summed = jnp.sum(parts_ref[...].reshape(8, 16, LANES), axis=0)
    weight = 1.0 / (summed * scale + EPSILON)
    gain = gain_ref[...]
    hr, hi = band_chain(bands_ref[...], delay_ref[...], x_ref[0, 0], step)
    outer = packed_sources(gain[0:2], gain[2:4])
    sources = [
        packed_sources(
            jnp.concatenate([hr[k : k + 1], hr[8 + k : 9 + k]], axis=0),
            jnp.concatenate([hi[k : k + 1], hi[8 + k : 9 + k]], axis=0),
        )
        for k in range(8)
    ]
    for inner in range(2):
        outer_pr, outer_pi, outer_qr, outer_qi = packed_lookup(outer, mine_ref, inner)
        total = None
        for k in range(8):
            slots = scratch[3 * ((2 * k + inner) % 4) : 3 * ((2 * k + inner) % 4) + 3]
            cr, ci, power = packed_stats(
                data_ref, cell_base(k, inner), weight[inner * 8 : inner * 8 + 8], slots
            )
            ar, ai, br, bi = packed_lookup(sources[k], mine_ref, inner)
            pr, pi = cmul(outer_pr, outer_pi, ar, ai)
            qr, qi = cmul(outer_qr, outer_qi, br, bi)
            rr = cr - (pr * qr + pi * qi) * power
            ri = ci - (pi * qr - pr * qi) * power
            left_re, left_im = conj_mul(ar, ai, *cmul(qr, qi, rr, ri))
            right_re, right_im = conj_mul(br, bi, *conj_mul(rr, ri, pr, pi))
            terms = [
                left_re,
                left_im,
                (ar * ar + ai * ai) * ((qr * qr + qi * qi) * power),
                right_re,
                right_im,
                (br * br + bi * bi) * ((pr * pr + pi * pi) * power),
            ]
            total = terms if total is None else [a + b for a, b in zip(total, terms)]
        split_into(left_ref, pl.ds(inner * LANES, LANES), jnp.concatenate(total, axis=0))
    sums = joined(contract(left_ref[...], hot_ref[...]))
    row = lax.broadcasted_iota(jnp.int32, (8, LANES), 0)
    chosen = [
        jnp.sum(jnp.where(row == z_ref[0, 0], weight[h * 8 : h * 8 + 8], 0.0), axis=0, keepdims=True)
        for h in range(2)
    ]
    copies(jnp.concatenate(antenna_rows(sums) + chosen, axis=0), send_ref)


def stepped(numerator_re, numerator_im, denominator):
    return jnp.concatenate(
        [DAMPING * numerator_re / denominator, DAMPING * numerator_im / denominator], axis=0
    )


def mix_kernel(data_ref, received_ref, index_ref, gain_ref, new_ref, mix_ref, kept_ref, *scratch):
    summed = jnp.sum(received_ref[...].reshape(64, 8, LANES), axis=0)
    gain = gain_ref[...] + stepped(summed[0:2], summed[2:4], summed[4:6])
    new_ref[...] = gain
    sources = packed_sources(gain[0:2], gain[2:4])
    pairs = index_ref.shape[0] // 16
    baselines = kept_ref.shape[1]
    for pair in range(pairs):
        folded = scratch[12 + 3 * (pair % 2) : 15 + 3 * (pair % 2)]
        for half in range(2):
            block = pair + half * pairs
            weight = received_ref[pl.ds(block // 2 * 64 + 6 + block % 2, 8, stride=8), :]
            width = min(LANES, baselines - block * LANES)
            kept_ref[:, pl.ds(block * LANES, width)] = weight[:, 0:width]
            slot = (2 * pair + half) % 4
            cr, ci, power = packed_stats(
                data_ref,
                cell_base(block // 2, block % 2),
                weight,
                scratch[3 * slot : 3 * slot + 3],
            )
            pr, pi, qr, qi = packed_lookup(sources, index_ref, block)
            er, ei = conj_mul(pr, pi, qr, qi)
            ar, ai = cmul(er, ei, cr, ci)
            power = (pr * pr + pi * pi) * ((qr * qr + qi * qi) * power)
            for ref, value in zip(folded, (ar, ai, power)):
                ref[pl.ds(half * 8, 8), :] = value
        lanes = pl.ds(pair * LANES, LANES)
        for slot, ref in enumerate(folded):
            mix_ref[slot * 8 : slot * 8 + 8, lanes] = (
                ref[pl.ds(0, 8, stride=2), :] + ref[pl.ds(1, 8, stride=2), :]
            )


def solve_kernel(
    mix_ref, index_ref, hot_ref, band_ref, delay_ref, x_ref, new_ref, send_ref, left_ref
):
    x = x_ref[0, 0]
    angle = TURN * delay_ref[...] * x
    kr, ki = jnp.cos(angle), jnp.sin(angle)
    band = band_ref[...]
    hr, hi = cmul(band[0:2], band[2:4], kr, ki)
    ur, ui, w = paired_sums(mix_ref, index_ref, hot_ref, hr, hi, left_ref)
    nr, ni = conj_mul(kr, ki, ur, ui)
    band = band + stepped(nr, ni, (kr * kr + ki * ki) * w)
    new_ref[...] = band
    hr, hi = cmul(band[0:2], band[2:4], kr, ki)
    ur, ui, w = paired_sums(mix_ref, index_ref, hot_ref, hr, hi, left_ref)
    turning = TURN * x
    n = turning * (hr * ui - hi * ur)
    d = (turning * turning) * ((hr * hr + hi * hi) * w)
    low = low_half((1, LANES))
    four = [jnp.where(low, p[0:1], p[1:2]) for p in (n, d, band[0:2], band[2:4])]
    copies(jnp.concatenate(four * 2, axis=0), send_ref)


def call(body, outs, operands, scratch=()):
    vmem = pl.BlockSpec(memory_space=pltpu.VMEM)
    smem = pl.BlockSpec(memory_space=pltpu.SMEM)
    return pl.pallas_call(
        body,
        out_shape=tuple(
            o if isinstance(o, jax.ShapeDtypeStruct) else jax.ShapeDtypeStruct(o, F32)
            for o in outs
        ),
        in_specs=[smem if o.shape == (1, 1) else vmem for o in operands],
        out_specs=tuple(vmem for _ in outs),
        scratch_shapes=list(scratch),
        compiler_params=pltpu.CompilerParams(vmem_limit_bytes=12 << 20),
    )(*operands)


def exchange(array, axis):
    devices = lax.axis_size(axis)
    chunks = array.reshape(devices, 1, -1)
    return lax.all_to_all(chunks, axis, 0, 0, tiled=True).reshape(array.shape)


def pair_total(array):
    for axis in ("tm_1", "tm_0"):
        array = array + lax.ppermute(array, axis, [(0, 1), (1, 0)])
    return array


def shards(
    visibilities, sky_model, gain_time, gain_band, delay_start, first_antenna, second_antenna
):
    antennas = gain_time.shape[-1]
    baselines = visibilities.shape[4]
    blocks = 2 * lax.axis_size(YX)
    padded = blocks * LANES
    times = visibilities.shape[2]
    channels = lax.axis_size(FREQ)
    z = lax.axis_index(Z)

    def offset_of(channel):
        return ((channel.astype(F32) + 0.5) / channels - 0.5).reshape(1, 1)

    x, x0 = offset_of(lax.axis_index(FREQ)), offset_of(z)
    step = lax.axis_size(Z) / channels
    z = z.astype(jnp.int32).reshape(1, 1)
    member = lax.axis_index(YX).astype(jnp.int32).reshape(1, 1)

    def ints(*shape):
        return jax.ShapeDtypeStruct(shape, jnp.int32)

    def marks(*shape):
        return jax.ShapeDtypeStruct(shape, jnp.bfloat16)

    def rows(count):
        return (count, LANES)

    (data,) = call(
        arrange_kernel,
        [rows(8 * CHUNK)],
        (visibilities.reshape(-1, baselines), sky_model.reshape(-1, baselines), gain_band),
    )
    gain, band, delay, index, hot, mine, mine_hot = call(
        table_kernel,
        [
            rows(4),
            rows(4),
            rows(2),
            ints(blocks * 8, LANES),
            marks(4 * HALF, padded // 2),
            ints(16, LANES),
            marks(2 * HALF, 2 * LANES),
        ],
        (
            first_antenna.reshape(1, -1),
            second_antenna.reshape(1, -1),
            gain_time,
            gain_band,
            delay_start,
            member,
        ),
    )
    group = exchange(data, YX)
    wide = pltpu.VMEM((144, 2 * LANES), jnp.bfloat16)
    half_wide = pltpu.VMEM((144, padded // 2), jnp.bfloat16)
    tall, short = pltpu.VMEM((32, LANES), F32), pltpu.VMEM((16, LANES), F32)
    for sweep in range(SWEEPS):
        if sweep == 0:
            power, bands = call(
                functools.partial(first_kernel, step),
                [rows(128), rows(32)],
                (group, mine, gain, delay, x0),
            )
        else:
            power, bands, delay = call(
                functools.partial(next_kernel, step),
                [rows(128), rows(32), rows(2)],
                (group, mine, gain, delay, received, z, x0),
            )
        (send,) = call(
            functools.partial(time_kernel, 1.0 / (4 * channels), step),
            [rows(512)],
            (group, exchange(power, Z), mine, mine_hot, gain, bands, delay, z, x0),
            [wide] + [tall] * 12,
        )
        outs, scratch = [rows(4), (24, padded // 2)], [tall] * 12 + [short] * 6
        if sweep < SWEEPS - 1:
            scratch = [pltpu.VMEM((times, baselines), F32)] + scratch
        else:
            outs = outs + [(times, baselines)]
        gain, mix, *kept = call(
            mix_kernel, outs, (data, exchange(send, FREQ), index, gain), scratch
        )
        band, send = call(
            solve_kernel,
            [rows(4), rows(256)],
            (pair_total(mix), index, hot, band, delay, x),
            (half_wide,),
        )
        received = exchange(send, FREQ)
    residual, delay = call(
        last_kernel,
        [(PLANES, padded), rows(2)],
        (data, index, gain, band, delay, received, x),
    )
    return (
        gain.reshape(gain_time.shape),
        band[:, :antennas].reshape(gain_band.shape),
        delay[:, :antennas],
        kept[0],
        residual[:, :baselines].reshape(visibilities.shape),
    )


def solution(mesh):
    split = Mesh(
        mesh.devices.reshape(2, 2, 4, 2, 8), ("tm_0", "tm_1", "freq_0", "freq_1", "freq_2")
    )
    placed = (
        P(None, None, TM, FREQ, None),
        P(None, None, TM, FREQ, None),
        P(None, None, TM, None),
        P(None, None, FREQ, None),
        P(),
        P(),
        P(),
    )
    return jax.shard_map(
        shards,
        mesh=split,
        in_specs=placed,
        out_specs=(
            P(None, None, TM, None),
            P(None, None, FREQ, None),
            P(),
            P(TM, None),
            P(None, None, TM, FREQ, None),
        ),
        check_vma=False,
    )
```

time: 165 us -> 150 us (0.909)
  blocking collectives: 123 us -> 79.6 us
  waiting for transfers between devices: 20.9 us -> 38.9 us
  starting transfers between devices: 7.84 us -> 13.9 us
  Pallas kernels: 7.29 us -> 12.2 us
    all_to_all x9 -> x5, blocking collectives: 123 us -> 79.6 us  [exchange(): return lax.all_to_all(chunks, axis, 0, 0, tiled=True).reshape(array.shape)]
    all_to_all x1 -> x2, waiting for transfers between devices: 11.5 us -> 29.4 us  [exchange(): return lax.all_to_all(chunks, axis, 0, 0, tiled=True).reshape(array.shape)]
    all_to_all x1 -> x2, starting transfers between devices: 4.62 us -> 10.8 us  [exchange(): return lax.all_to_all(chunks, axis, 0, 0, tiled=True).reshape(array.shape)]
    pallas_call x13 -> x11, Pallas kernels: 7.29 us -> 12.2 us  [call(): pl.pallas_call(body, out_shape=tuple((o if isinstance(o, jax.ShapeDtypeSt...]
  transfers between devices with their start and end apart: 5 -> 6, of which waited for: 5 -> 6; matrix products, arithmetic and copies ran while one was open for 0% -> 0% of each run, Pallas kernels for 0% -> 0%
where the time goes in v2:
time: 150 us
  blocking collectives  79.6 us (53%)
  waiting for transfers between devices  38.9 us (26%)
  starting transfers between devices  13.9 us (9%)
  Pallas kernels  12.2 us (8%)
  local copies, waits for them, and re-layouts  4.13 us (3%)
    all_to_all x5, blocking collectives, exchange(): return lax.all_to_all(chunks, axis, 0, 0, tiled=True).reshape(array.shape)  79.6 us
    all_to_all x2, waiting for transfers between devices, exchange(): return lax.all_to_all(chunks, axis, 0, 0, tiled=True).reshape(array.shape)  29.4 us
    pallas_call x11, Pallas kernels, call(): pl.pallas_call(body, out_shape=tuple((o if isinstance(o, jax.ShapeDtypeSt...  12.2 us
    all_to_all x2, starting transfers between devices, exchange(): return lax.all_to_all(chunks, axis, 0, 0, tiled=True).reshape(array.shape)  10.8 us
    ppermute x4, waiting for transfers between devices, pair_total(): array = array + lax.ppermute(array, axis, [(0, 1), (1, 0)])  9.44 us
    unnamed x17, local copies, waits for them, and re-layouts  3.46 us
    ppermute x4, starting transfers between devices, pair_total(): array = array + lax.ppermute(array, axis, [(0, 1), (1, 0)])  3.12 us
  transfers between devices with their start and end apart: 6, of which 6 were waited for; matrix products, arithmetic and copies ran while one was open for 0% of the time, Pallas kernels for 0%

profile of v2, /device:TPU:2, one launch (start us, length us, event | category | flops | bytes accessed | tf_op | source)
XLA Modules:
  0.0 149.5 jit_solution(14316301857269592797)
XLA Ops:
  0.7 1.3 copy.23
  2.1 1.1 shard_map.110.data_ref
  3.2 6.2 %all-to-all-start = ((f32[8,1,33792]{2,1,0:T(1,128)}), f32[8,1,33792]{2,1,0:T(1,128)S(1)}, u32[]{:S(2)}, u32[]{:S(2)}) async-start(f32[8,1,33792]{2,1,0:T(1,128)} %bitcast), calls=%async_computation | async-start | bytes 2162688 | tf_op jit(solution)/shard_map/all_to_all | solution.py:557
  9.6 17.4 %all-to-all-done = f32[8,1,33792]{2,1,0:T(1,128)S(1)} async-done(((f32[8,1,33792]{2,1,0:T(1,128)}), f32[8,1,33792]{2,1,0:T(1,128)S(1)}, u32[]{:S(2)}, u32[]{:S(2)}) %all-to-all-start) | async-done | bytes 1081376 | tf_op jit(solution)/shard_map/all_to_all | solution.py:557
  27.4 16.6 %all_to_all.35 = f32[8,1,2048]{2,1,0:T(1,128)S(1)} all-to-all(f32[8,1,2048]{2,1,0:T(1,128)S(1)} %bitcast.46), channel_id=1, replica_groups=mesh['tm_0'=2,'tm_1'=2,'freq_0'=4,'freq_1'=2,'freq_2'=8] {'freq_2'}, dimensions={0} | all-to-all | bytes 131072 | tf_op jit(solution)/shard_map/all_to_all | solution.py:557
  44.6 17.7 %all_to_all.36 = f32[64,1,1024]{2,1,0:T(1,128)S(1)} all-to-all(f32[64,1,1024]{2,1,0:T(1,128)S(1)} %bitcast.38), channel_id=1, replica_groups=mesh['tm_0'=2,'tm_1'=2,'freq_0'=4,'freq_1'=2,'freq_2'=8] {'freq_0','freq..., dimensions={0} | all-to-all | bytes 524288 | tf_op jit(solution)/shard_map/all_to_all | solution.py:557
  62.4 1.6 %shard_map.114 = (f32[4,128]{1,0:T(4,128)S(1)}, f32[24,1024]{1,0:T(8,128)S(1)}) custom-call(f32[2112,128]{1,0:T(8,128)} %shard_map.110.data_ref, f32[512,128]{1,0:T(8,128)S(1)} %bitcast.37, s32[128,128]{1,0:T(8,128)S(1)} %get-tuple-element.34.index_ref, f32[4,128]{1,0:T(4,128)S(1)} %get-tuple-element.29.gain_ref), custom_call_target="tpu_custom_call" | custom-call | tf_op jit(solution)/shard_map/pallas_call | solution.py:541
  64.0 1.3 collective-permute-done
  65.3 1.5 %collective-permute-start.1 = (f32[24,1024]{1,0:T(8,128)S(1)}, f32[24,1024]{1,0:T(8,128)S(1)}, u32[]{:S(2)}, u32[]{:S(2)}) collective-permute-start(f32[24,1024]{1,0:T(8,128)S(1)} %add.31), channel_id=1, source_target_pairs={{0,128},{128,0},{1,129},{129,1},{2,130},{130,2},{3,131},{131,3},{4... | collective-permute-start | bytes 294920 | tf_op jit(solution)/shard_map/ppermute | solution.py:562
  66.8 3.4 %collective-permute-done.1 = f32[24,1024]{1,0:T(8,128)S(1)} collective-permute-done((f32[24,1024]{1,0:T(8,128)S(1)}, f32[24,1024]{1,0:T(8,128)S(1)}, u32[]{:S(2)}, u32[]{:S(2)}) %collective-permute-start.1) | collective-permute-done | bytes 98336 | tf_op jit(solution)/shard_map/ppermute | solution.py:562
  70.3 1.3 shard_map.115
  71.6 16.9 %all_to_all.37 = f32[64,1,512]{2,1,0:T(1,128)S(1)} all-to-all(f32[64,1,512]{2,1,0:T(1,128)S(1)} %bitcast.44), channel_id=1, replica_groups=mesh['tm_0'=2,'tm_1'=2,'freq_0'=4,'freq_1'=2,'freq_2'=8] {'freq_0','freq..., dimensions={0} | all-to-all | bytes 262144 | tf_op jit(solution)/shard_map/all_to_all | solution.py:557
  89.0 10.8 %all_to_all.38 = f32[8,1,2048]{2,1,0:T(1,128)S(1)} all-to-all(f32[8,1,2048]{2,1,0:T(1,128)S(1)} %bitcast.45), channel_id=1, replica_groups=mesh['tm_0'=2,'tm_1'=2,'freq_0'=4,'freq_1'=2,'freq_2'=8] {'freq_2'}, dimensions={0} | all-to-all | bytes 131072 | tf_op jit(solution)/shard_map/all_to_all | solution.py:557
  100.4 17.5 %all_to_all.39 = f32[64,1,1024]{2,1,0:T(1,128)S(1)} all-to-all(f32[64,1,1024]{2,1,0:T(1,128)S(1)} %bitcast.35), channel_id=1, replica_groups=mesh['tm_0'=2,'tm_1'=2,'freq_0'=4,'freq_1'=2,'freq_2'=8] {'freq_0','freq..., dimensions={0} | all-to-all | bytes 524288 | tf_op jit(solution)/shard_map/all_to_all | solution.py:557
  117.9 2.1 %shard_map.118 = (f32[4,128]{1,0:T(4,128)S(1)}, f32[24,1024]{1,0:T(8,128)S(1)}, f32[8,2016]{1,0:T(8,128)}) custom-call(f32[2112,128]{1,0:T(8,128)} %shard_map.110.data_ref, f32[512,128]{1,0:T(8,128)S(1)} %bitcast.36, s32[128,128]{1,0:T(8,128)S(1)} %get-tuple-element.34.index_ref, f32[4,128]{1,0:T(4,128)S(1)} %get-tuple-element.35.gain_ref), custom_call_target="tpu_custom_call" | custom-call | tf_op jit(solution)/shard_map/pallas_call | solution.py:541
  120.0 1.3 collective-permute-done.2
  121.3 1.5 %collective-permute-start.3 = (f32[24,1024]{1,0:T(8,128)S(1)}, f32[24,1024]{1,0:T(8,128)S(1)}, u32[]{:S(2)}, u32[]{:S(2)}) collective-permute-start(f32[24,1024]{1,0:T(8,128)S(1)} %add.36), channel_id=1, source_target_pairs={{0,128},{128,0},{1,129},{129,1},{2,130},{130,2},{3,131},{131,3},{4... | collective-permute-start | bytes 294920 | tf_op jit(solution)/shard_map/ppermute | solution.py:562
  122.9 3.4 %collective-permute-done.3 = f32[24,1024]{1,0:T(8,128)S(1)} collective-permute-done((f32[24,1024]{1,0:T(8,128)S(1)}, f32[24,1024]{1,0:T(8,128)S(1)}, u32[]{:S(2)}, u32[]{:S(2)}) %collective-permute-start.3) | collective-permute-done | bytes 98336 | tf_op jit(solution)/shard_map/ppermute | solution.py:562
  126.3 2.0 %shard_map.119 = (f32[4,128]{1,0:T(4,128)}, f32[256,128]{1,0:T(8,128)}) custom-call(f32[24,1024]{1,0:T(8,128)S(1)} %add.37.mix_ref, s32[128,128]{1,0:T(8,128)S(1)} %get-tuple-element.34.index_ref, bf16[256,1024]{1,0:T(8,128)(2,1)S(1)} %get-tuple-element.37.hot_ref, f32[4,128]{1,0:T(4,128)S(1)} %get-tuple-element.45.band_ref, ...), custom_call_target="tpu_custom_call" | custom-call | tf_op jit(solution)/shard_map/pallas_call | solution.py:541
  128.3 4.6 %all-to-all-start.6 = ((f32[64,1,512]{2,1,0:T(1,128)}), f32[64,1,512]{2,1,0:T(1,128)S(1)}, u32[]{:S(2)}, u32[]{:S(2)}) async-start(f32[64,1,512]{2,1,0:T(1,128)} %bitcast.20), calls=%async_computation.6 | async-start | bytes 262144 | tf_op jit(solution)/shard_map/all_to_all | solution.py:557
  133.6 12.0 %all-to-all-done.6 = f32[64,1,512]{2,1,0:T(1,128)S(1)} async-done(((f32[64,1,512]{2,1,0:T(1,128)}), f32[64,1,512]{2,1,0:T(1,128)S(1)}, u32[]{:S(2)}, u32[]{:S(2)}) %all-to-all-start.6) | async-done | bytes 131104 | tf_op jit(solution)/shard_map/all_to_all | solution.py:557
  145.6 0.7 copy-done.4
  146.3 1.9 %shard_map.120 = (f32[64,2048]{1,0:T(8,128)S(1)}, f32[2,128]{1,0:T(2,128)}) custom-call(f32[2112,128]{1,0:T(8,128)} %shard_map.110.data_ref, s32[128,128]{1,0:T(8,128)S(1)} %get-tuple-element.34.index_ref, f32[4,128]{1,0:T(4,128)S(1)} %get-tuple-element.43.gain_ref, f32[4,128]{1,0:T(4,128)S(1)} %copy-done.4, f32[2,128]{1,0:T(2,128)S(1)} %get-tuple-element.42.delay_ref, ...), custom_call_target="tpu_custom_call" | custom-call | tf_op jit(solution)/shard_map/pallas_call | solution.py:541
  148.2 1.3 copy.22
  (26 shorter events, 3.3 us)
Async XLA Ops:
  0.6 1.3 copy-start.6
  0.6 1.5 copy-start
  3.2 6.2 %copy-start.1 = (s32[2016]{0:T(1024)S(1)}, s32[2016]{0:T(1024)}, u32[]{:S(2)}) copy-start(s32[2016]{0:T(1024)} %param.12) | copy-start | bytes 24196
  3.2 6.2 %copy-start.2 = (s32[2016]{0:T(1024)S(1)}, s32[2016]{0:T(1024)}, u32[]{:S(2)}) copy-start(s32[2016]{0:T(1024)} %param.13) | copy-start | bytes 24196
  3.2 6.2 %copy-start.3 = (f32[2,2,2,64]{3,2,1,0:T(2,128)S(1)}, f32[2,2,2,64]{3,2,1,0:T(2,128)}, u32[]{:S(2)}) copy-start(f32[2,2,2,64]{3,2,1,0:T(2,128)} %time_ref.1) | copy-start | bytes 6148
  3.2 6.2 %copy-start.5 = (f32[2,64]{1,0:T(2,128)S(1)}, f32[2,64]{1,0:T(2,128)}, u32[]{:S(2)}) copy-start(f32[2,64]{1,0:T(2,128)} %start_ref.1) | copy-start | bytes 1540
  3.2 23.8 %all-to-all-start = ((f32[8,1,33792]{2,1,0:T(1,128)}), f32[8,1,33792]{2,1,0:T(1,128)S(1)}, u32[]{:S(2)}, u32[]{:S(2)}) async-start(f32[8,1,33792]{2,1,0:T(1,128)} %bitcast), calls=%async_computation | async-start | bytes 2162688 | tf_op jit(solution)/shard_map/all_to_all | solution.py:557
  63.9 1.4 collective-permute-start
  65.3 4.9 %collective-permute-start.1 = (f32[24,1024]{1,0:T(8,128)S(1)}, f32[24,1024]{1,0:T(8,128)S(1)}, u32[]{:S(2)}, u32[]{:S(2)}) collective-permute-start(f32[24,1024]{1,0:T(8,128)S(1)} %add.31), channel_id=1, source_target_pairs={{0,128},{128,0},{1,129},{129,1},{2,130},{130,2},{3,131},{131,3},{4... | collective-permute-start | bytes 294920 | tf_op jit(solution)/shard_map/ppermute | solution.py:562
  120.0 1.3 collective-permute-start.2
  121.3 4.9 %collective-permute-start.3 = (f32[24,1024]{1,0:T(8,128)S(1)}, f32[24,1024]{1,0:T(8,128)S(1)}, u32[]{:S(2)}, u32[]{:S(2)}) collective-permute-start(f32[24,1024]{1,0:T(8,128)S(1)} %add.36), channel_id=1, source_target_pairs={{0,128},{128,0},{1,129},{129,1},{2,130},{130,2},{3,131},{131,3},{4... | collective-permute-start | bytes 294920 | tf_op jit(solution)/shard_map/ppermute | solution.py:562
  128.3 17.3 %all-to-all-start.6 = ((f32[64,1,512]{2,1,0:T(1,128)}), f32[64,1,512]{2,1,0:T(1,128)S(1)}, u32[]{:S(2)}, u32[]{:S(2)}) async-start(f32[64,1,512]{2,1,0:T(1,128)} %bitcast.20), calls=%async_computation.6 | async-start | bytes 262144 | tf_op jit(solution)/shard_map/all_to_all | solution.py:557
  145.6 0.7 copy-start.4

commit v3 on v2

--- a/solution.py
+++ b/solution.py
@@ -17,6 +17,8 @@
 HALF = 64
 PLANES = 64
 CHUNK = 4 * PLANES + 8
+CHANNELS = 64
+DEEP = 8
 FREQ = ("freq_0", "freq_1", "freq_2")
 TM = ("tm_0", "tm_1")
 YX = ("freq_0", "freq_1")
@@ -83,6 +85,18 @@
 
 def time_offset():
     return jnp.where(lax.broadcasted_iota(jnp.int32, (8, LANES), 0) >= 4, HALF, 0)
+
+
+def offset_of(channel):
+    return (channel.astype(F32) + 0.5) * (1.0 / CHANNELS) - 0.5
+
+
+def own_offset(own_ref):
+    return offset_of(own_ref[0, 0])
+
+
+def depth(own_ref):
+    return lax.rem(own_ref[0, 0], DEEP)
 
 
 def stacked(pair):
@@ -131,9 +145,11 @@
     return jnp.concatenate([left, right], axis=1)
 
 
-def arrange_kernel(v_ref, s_ref, channel_ref, data_ref):
+def arrange_kernel(v_ref, s_ref, *refs):
+    data_ref = refs[6]
+    tables(*refs[:6], *refs[7:])
     baselines = v_ref.shape[1]
-    band = own_band(channel_ref)
+    band = own_band(refs[3])
     for chunk in range(8):
         for inner in range(2):
             at = (2 * chunk + inner) * LANES
@@ -152,13 +168,13 @@
     return side_by_side(band, band)
 
 
-def table_kernel(
+def tables(
     first_ref,
     second_ref,
     time_ref,
     channel_ref,
     start_ref,
-    member_ref,
+    own_ref,
     gain_ref,
     band_ref,
     delay_ref,
@@ -197,7 +213,7 @@
         for side in range(2):
             rows = pl.ds((half * 2 + side) * HALF, HALF)
             hot_ref[rows, pl.ds(at * LANES, LANES)] = marks(index_ref, block, side)
-    mine_ref[...] = index_ref[pl.ds(pl.multiple_of(member_ref[0, 0] * 16, 16), 16), :]
+    mine_ref[...] = index_ref[pl.ds(pl.multiple_of(lax.div(own_ref[0, 0], DEEP) * 16, 16), 16), :]
     for inner in range(2):
         for side in range(2):
             mine_hot_ref[pl.ds(side * HALF, HALF), pl.ds(inner * LANES, LANES)] = marks(
@@ -206,15 +222,16 @@
 
 
 def first_kernel(
-    step, data_ref, mine_ref, gain_ref, delay_ref, x_ref, power_ref, bands_ref
+    step, data_ref, mine_ref, gain_ref, delay_ref, own_ref, power_ref, bands_ref
 ):
+    x0 = offset_of(depth(own_ref))
     at = [k * CHUNK + 4 * PLANES for k in range(8)]
     bands = jnp.concatenate(
         [data_ref[at[k] + r : at[k] + r + 1, :] for r in range(4) for k in range(8)], axis=0
     )
     bands_ref[...] = bands
     noise_into(
-        data_ref, mine_ref, gain_ref[...], bands, delay_ref[...], x_ref[0, 0], step, power_ref
+        data_ref, mine_ref, gain_ref[...], bands, delay_ref[...], x0, step, power_ref
     )
 
 
@@ -225,15 +242,14 @@
     gain_ref,
     delay_ref,
     received_ref,
-    z_ref,
-    x_ref,
+    own_ref,
     power_ref,
     bands_ref,
     new_ref,
 ):
     delay = delay_step(received_ref, delay_ref[...])
     new_ref[...] = delay
-    z = z_ref[0, 0]
+    z = depth(own_ref)
     re, im = [], []
     odd = z % 2 == 1
     for k in range(8):
@@ -252,15 +268,36 @@
         bands += [jnp.where(low, value, turned), jnp.where(low, turned, value)]
     bands = jnp.concatenate(bands, axis=0)
     bands_ref[...] = bands
-    noise_into(data_ref, mine_ref, gain_ref[...], bands, delay, x_ref[0, 0], step, power_ref)
+    x0 = offset_of(z)
+    noise_into(data_ref, mine_ref, gain_ref[...], bands, delay, x0, step, power_ref)
 
 
 def last_kernel(
-    data_ref, index_ref, gain_ref, band_ref, delay_ref, received_ref, x_ref, out_ref, new_ref
+    data_ref,
+    index_ref,
+    gain_ref,
+    band_ref,
+    delay_ref,
+    weight_ref,
+    received_ref,
+    own_ref,
+    out_ref,
+    time_ref,
+    channel_ref,
+    last_ref,
+    kept_ref,
 ):
     delay = delay_step(received_ref, delay_ref[...])
-    new_ref[...] = delay
-    _, _, (gr, gi) = chain(gain_ref[...], band_ref[...], delay, x_ref[0, 0])
+    last_ref[...] = delay[:, 0:HALF]
+    kept_ref[...] = weight_ref[...]
+    gain = gain_ref[...]
+    turned = half_roll(jnp.concatenate([gain, gain], axis=0))
+    for row in range(4):
+        part, a = row // 2, row % 2
+        time_ref[part, a, 0:1] = gain[row : row + 1, 0:HALF]
+        time_ref[part, a, 1:2] = turned[row : row + 1, 0:HALF]
+        channel_ref[part, a] = band_ref[row : row + 1, 0:HALF]
+    _, _, (gr, gi) = chain(gain_ref[...], band_ref[...], delay, own_offset(own_ref))
     offset = time_offset()
     sources = [(fill(gr[a : a + 1]), fill(gi[a : a + 1])) for a in range(2)]
     for block in range(index_ref.shape[0] // 8):
@@ -421,8 +458,7 @@
     gain_ref,
     bands_ref,
     delay_ref,
-    z_ref,
-    x_ref,
+    own_ref,
     send_ref,
     left_ref,
     *scratch,
@@ -430,7 +466,8 @@
     summed = jnp.sum(parts_ref[...].reshape(8, 16, LANES), axis=0)
     weight = 1.0 / (summed * scale + EPSILON)
     gain = gain_ref[...]
-    hr, hi = band_chain(bands_ref[...], delay_ref[...], x_ref[0, 0], step)
+    z = depth(own_ref)
+    hr, hi = band_chain(bands_ref[...], delay_ref[...], offset_of(z), step)
     outer = packed_sources(gain[0:2], gain[2:4])
     sources = [
         packed_sources(
@@ -467,7 +504,7 @@
     sums = joined(contract(left_ref[...], hot_ref[...]))
     row = lax.broadcasted_iota(jnp.int32, (8, LANES), 0)
     chosen = [
-        jnp.sum(jnp.where(row == z_ref[0, 0], weight[h * 8 : h * 8 + 8], 0.0), axis=0, keepdims=True)
+        jnp.sum(jnp.where(row == z, weight[h * 8 : h * 8 + 8], 0.0), axis=0, keepdims=True)
         for h in range(2)
     ]
     copies(jnp.concatenate(antenna_rows(sums) + chosen, axis=0), send_ref)
@@ -514,9 +551,9 @@
 
 
 def solve_kernel(
-    mix_ref, index_ref, hot_ref, band_ref, delay_ref, x_ref, new_ref, send_ref, left_ref
+    mix_ref, index_ref, hot_ref, band_ref, delay_ref, own_ref, new_ref, send_ref, left_ref
 ):
-    x = x_ref[0, 0]
+    x = own_offset(own_ref)
     angle = TURN * delay_ref[...] * x
     kr, ki = jnp.cos(angle), jnp.sin(angle)
     band = band_ref[...]
@@ -572,15 +609,8 @@
     padded = blocks * LANES
     times = visibilities.shape[2]
     channels = lax.axis_size(FREQ)
-    z = lax.axis_index(Z)
-
-    def offset_of(channel):
-        return ((channel.astype(F32) + 0.5) / channels - 0.5).reshape(1, 1)
-
-    x, x0 = offset_of(lax.axis_index(FREQ)), offset_of(z)
+    own = lax.axis_index(FREQ).astype(jnp.int32).reshape(1, 1)
     step = lax.axis_size(Z) / channels
-    z = z.astype(jnp.int32).reshape(1, 1)
-    member = lax.axis_index(YX).astype(jnp.int32).reshape(1, 1)
 
     def ints(*shape):
         return jax.ShapeDtypeStruct(shape, jnp.int32)
@@ -591,14 +621,10 @@
     def rows(count):
         return (count, LANES)
 
-    (data,) = call(
+    data, gain, band, delay, index, hot, mine, mine_hot = call(
         arrange_kernel,
-        [rows(8 * CHUNK)],
-        (visibilities.reshape(-1, baselines), sky_model.reshape(-1, baselines), gain_band),
-    )
-    gain, band, delay, index, hot, mine, mine_hot = call(
-        table_kernel,
         [
+            rows(8 * CHUNK),
             rows(4),
             rows(4),
             rows(2),
@@ -608,12 +634,14 @@
             marks(2 * HALF, 2 * LANES),
         ],
         (
+            visibilities.reshape(-1, baselines),
+            sky_model.reshape(-1, baselines),
             first_antenna.reshape(1, -1),
             second_antenna.reshape(1, -1),
             gain_time,
             gain_band,
             delay_start,
-            member,
+            own,
         ),
     )
     group = exchange(data, YX)
@@ -625,18 +653,18 @@
             power, bands = call(
                 functools.partial(first_kernel, step),
                 [rows(128), rows(32)],
-                (group, mine, gain, delay, x0),
+                (group, mine, gain, delay, own),
             )
         else:
             power, bands, delay = call(
                 functools.partial(next_kernel, step),
                 [rows(128), rows(32), rows(2)],
-                (group, mine, gain, delay, received, z, x0),
+                (group, mine, gain, delay, received, own),
             )
         (send,) = call(
             functools.partial(time_kernel, 1.0 / (4 * channels), step),
             [rows(512)],
-            (group, exchange(power, Z), mine, mine_hot, gain, bands, delay, z, x0),
+            (group, exchange(power, Z), mine, mine_hot, gain, bands, delay, own),
             [wide] + [tall] * 12,
         )
         outs, scratch = [rows(4), (24, padded // 2)], [tall] * 12 + [short] * 6
@@ -650,22 +678,16 @@
         band, send = call(
             solve_kernel,
             [rows(4), rows(256)],
-            (pair_total(mix), index, hot, band, delay, x),
+            (pair_total(mix), index, hot, band, delay, own),
             (half_wide,),
         )
         received = exchange(send, FREQ)
-    residual, delay = call(
+    residual, *small = call(
         last_kernel,
-        [(PLANES, padded), rows(2)],
-        (data, index, gain, band, delay, received, x),
-    )
-    return (
-        gain.reshape(gain_time.shape),
-        band[:, :antennas].reshape(gain_band.shape),
-        delay[:, :antennas],
-        kept[0],
-        residual[:, :baselines].reshape(visibilities.shape),
-    )
+        [(PLANES, padded), gain_time.shape, gain_band.shape, (2, antennas), (times, baselines)],
+        (data, index, gain, band, delay, kept[0], received, own),
+    )
+    return *small, residual[:, :baselines].reshape(visibilities.shape)
 
 
 def solution(mesh):

time: 150 us -> 143 us (0.953)
  blocking collectives: 79.6 us -> 120 us
  waiting for transfers between devices: 38.9 us -> 9.41 us
  starting transfers between devices: 13.9 us -> 3.22 us
  Pallas kernels: 12.2 us -> 6.69 us
    all_to_all x5 -> x7, blocking collectives: 79.6 us -> 120 us  [exchange(): return lax.all_to_all(chunks, axis, 0, 0, tiled=True).reshape(array.shape)]
    all_to_all x2 -> x0, waiting for transfers between devices: 29.4 us -> none  [exchange(): return lax.all_to_all(chunks, axis, 0, 0, tiled=True).reshape(array.shape)]
    all_to_all x2 -> x0, starting transfers between devices: 10.8 us -> none  [exchange(): return lax.all_to_all(chunks, axis, 0, 0, tiled=True).reshape(array.shape)]
    pallas_call x11 -> x10, Pallas kernels: 12.2 us -> 6.69 us  [call(): pl.pallas_call(body, out_shape=tuple((o if isinstance(o, jax.ShapeDtypeSt...]
    unnamed x17 -> x15, local copies, waits for them, and re-layouts: 3.46 us -> 2.77 us
  transfers between devices with their start and end apart: 6 -> 4, of which waited for: 6 -> 4; matrix products, arithmetic and copies ran while one was open for 0% -> 0% of each run, Pallas kernels for 0% -> 0%
where the time goes in v3:
time: 143 us
  blocking collectives  120 us (84%)
  waiting for transfers between devices  9.41 us (7%)
  Pallas kernels  6.69 us (5%)
  starting transfers between devices  3.22 us (2%)
  local copies, waits for them, and re-layouts  2.77 us (2%)
    all_to_all x7, blocking collectives, exchange(): return lax.all_to_all(chunks, axis, 0, 0, tiled=True).reshape(array.shape)  120 us
    ppermute x4, waiting for transfers between devices, pair_total(): array = array + lax.ppermute(array, axis, [(0, 1), (1, 0)])  9.41 us
    pallas_call x10, Pallas kernels, call(): pl.pallas_call(body, out_shape=tuple((o if isinstance(o, jax.ShapeDtypeSt...  6.69 us
    ppermute x4, starting transfers between devices, pair_total(): array = array + lax.ppermute(array, axis, [(0, 1), (1, 0)])  3.22 us
  transfers between devices with their start and end apart: 4, of which 4 were waited for; matrix products, arithmetic and copies ran while one was open for 0% of the time, Pallas kernels for 0%

profile of v3, /device:TPU:2, one launch (start us, length us, event | category | flops | bytes accessed | tf_op | source)
XLA Modules:
  0.0 143.1 jit_solution(14299592835372061552)
XLA Ops:
  0.7 1.3 copy.21
  2.4 23.6 %all_to_all.35 = f32[8,1,33792]{2,1,0:T(1,128)S(1)} all-to-all(f32[8,1,33792]{2,1,0:T(1,128)S(1)} %bitcast.25), channel_id=1, replica_groups=mesh['tm_0'=2,'tm_1'=2,'freq_0'=4,'freq_1'=2,'freq_2'=8] {'freq_0','freq..., dimensions={0} | all-to-all | bytes 2162688 | tf_op jit(solution)/shard_map/all_to_all | solution.py:594
  26.0 0.4 shard_map.111
  26.4 16.6 %all_to_all.36 = f32[8,1,2048]{2,1,0:T(1,128)S(1)} all-to-all(f32[8,1,2048]{2,1,0:T(1,128)S(1)} %bitcast.40), channel_id=1, replica_groups=mesh['tm_0'=2,'tm_1'=2,'freq_0'=4,'freq_1'=2,'freq_2'=8] {'freq_2'}, dimensions={0} | all-to-all | bytes 131072 | tf_op jit(solution)/shard_map/all_to_all | solution.py:594
  43.1 0.6 shard_map.112
  43.7 17.5 %all_to_all.37 = f32[64,1,1024]{2,1,0:T(1,128)S(1)} all-to-all(f32[64,1,1024]{2,1,0:T(1,128)S(1)} %bitcast.29), channel_id=1, replica_groups=mesh['tm_0'=2,'tm_1'=2,'freq_0'=4,'freq_1'=2,'freq_2'=8] {'freq_0','freq..., dimensions={0} | all-to-all | bytes 524288 | tf_op jit(solution)/shard_map/all_to_all | solution.py:594
  61.2 0.3 shard_map.113
  61.6 1.3 collective-permute-done
  62.9 1.5 %collective-permute-start.1 = (f32[24,1024]{1,0:T(8,128)S(1)}, f32[24,1024]{1,0:T(8,128)S(1)}, u32[]{:S(2)}, u32[]{:S(2)}) collective-permute-start(f32[24,1024]{1,0:T(8,128)S(1)} %add.20), channel_id=1, source_target_pairs={{0,128},{128,0},{1,129},{129,1},{2,130},{130,2},{3,131},{131,3},{4... | collective-permute-start | bytes 294920 | tf_op jit(solution)/shard_map/ppermute | solution.py:599
  64.4 3.4 %collective-permute-done.1 = f32[24,1024]{1,0:T(8,128)S(1)} collective-permute-done((f32[24,1024]{1,0:T(8,128)S(1)}, f32[24,1024]{1,0:T(8,128)S(1)}, u32[]{:S(2)}, u32[]{:S(2)}) %collective-permute-start.1) | collective-permute-done | bytes 98336 | tf_op jit(solution)/shard_map/ppermute | solution.py:599
  67.9 1.3 shard_map.114
  69.2 17.1 %all_to_all.38 = f32[64,1,512]{2,1,0:T(1,128)S(1)} all-to-all(f32[64,1,512]{2,1,0:T(1,128)S(1)} %bitcast.38), channel_id=1, replica_groups=mesh['tm_0'=2,'tm_1'=2,'freq_0'=4,'freq_1'=2,'freq_2'=8] {'freq_0','freq..., dimensions={0} | all-to-all | bytes 262144 | tf_op jit(solution)/shard_map/all_to_all | solution.py:594
  86.2 0.5 shard_map.115
  86.8 10.8 %all_to_all.39 = f32[8,1,2048]{2,1,0:T(1,128)S(1)} all-to-all(f32[8,1,2048]{2,1,0:T(1,128)S(1)} %bitcast.39), channel_id=1, replica_groups=mesh['tm_0'=2,'tm_1'=2,'freq_0'=4,'freq_1'=2,'freq_2'=8] {'freq_2'}, dimensions={0} | all-to-all | bytes 131072 | tf_op jit(solution)/shard_map/all_to_all | solution.py:594
  97.5 0.6 shard_map.116
  98.1 17.5 %all_to_all.40 = f32[64,1,1024]{2,1,0:T(1,128)S(1)} all-to-all(f32[64,1,1024]{2,1,0:T(1,128)S(1)} %bitcast.28), channel_id=1, replica_groups=mesh['tm_0'=2,'tm_1'=2,'freq_0'=4,'freq_1'=2,'freq_2'=8] {'freq_0','freq..., dimensions={0} | all-to-all | bytes 524288 | tf_op jit(solution)/shard_map/all_to_all | solution.py:594
  115.6 0.3 shard_map.117
  116.1 1.3 collective-permute-done.2
  117.4 1.5 %collective-permute-start.3 = (f32[24,1024]{1,0:T(8,128)S(1)}, f32[24,1024]{1,0:T(8,128)S(1)}, u32[]{:S(2)}, u32[]{:S(2)}) collective-permute-start(f32[24,1024]{1,0:T(8,128)S(1)} %add.22), channel_id=1, source_target_pairs={{0,128},{128,0},{1,129},{129,1},{2,130},{130,2},{3,131},{131,3},{4... | collective-permute-start | bytes 294920 | tf_op jit(solution)/shard_map/ppermute | solution.py:599
  118.9 3.4 %collective-permute-done.3 = f32[24,1024]{1,0:T(8,128)S(1)} collective-permute-done((f32[24,1024]{1,0:T(8,128)S(1)}, f32[24,1024]{1,0:T(8,128)S(1)}, u32[]{:S(2)}, u32[]{:S(2)}) %collective-permute-start.3) | collective-permute-done | bytes 98336 | tf_op jit(solution)/shard_map/ppermute | solution.py:599
  122.3 1.3 shard_map.118
  123.6 17.1 %all_to_all.41 = f32[64,1,512]{2,1,0:T(1,128)S(1)} all-to-all(f32[64,1,512]{2,1,0:T(1,128)S(1)} %bitcast.37), channel_id=1, replica_groups=mesh['tm_0'=2,'tm_1'=2,'freq_0'=4,'freq_1'=2,'freq_2'=8] {'freq_0','freq..., dimensions={0} | all-to-all | bytes 262144 | tf_op jit(solution)/shard_map/all_to_all | solution.py:594
  140.7 1.0 shard_map.119
  141.8 1.3 copy.20
  (20 shorter events, 0.7 us)
Async XLA Ops:
  0.6 1.3 copy-start.5
  0.6 1.5 %copy-start.1 = (s32[2016]{0:T(1024)S(1)}, s32[2016]{0:T(1024)}, u32[]{:S(2)}) copy-start(s32[2016]{0:T(1024)} %param.13) | copy-start | bytes 24196
  0.7 1.5 %copy-start = (s32[2016]{0:T(1024)S(1)}, s32[2016]{0:T(1024)}, u32[]{:S(2)}) copy-start(s32[2016]{0:T(1024)} %param.12) | copy-start | bytes 24196
  0.7 1.5 %copy-start.4 = (f32[2,64]{1,0:T(2,128)S(1)}, f32[2,64]{1,0:T(2,128)}, u32[]{:S(2)}) copy-start(f32[2,64]{1,0:T(2,128)} %refs_4_.1) | copy-start | bytes 1540
  0.7 1.5 %copy-start.3 = (f32[2,2,1,64]{3,2,1,0:T(1,128)S(1)}, f32[2,2,1,64]{3,2,1,0:T(1,128)}, u32[]{:S(2)}) copy-start(f32[2,2,1,64]{3,2,1,0:T(1,128)} %refs_3_.1) | copy-start | bytes 3076
  0.7 1.5 %copy-start.2 = (f32[2,2,2,64]{3,2,1,0:T(2,128)S(1)}, f32[2,2,2,64]{3,2,1,0:T(2,128)}, u32[]{:S(2)}) copy-start(f32[2,2,2,64]{3,2,1,0:T(2,128)} %refs_2_.1) | copy-start | bytes 6148
  61.5 1.4 collective-permute-start
  62.9 4.9 %collective-permute-start.1 = (f32[24,1024]{1,0:T(8,128)S(1)}, f32[24,1024]{1,0:T(8,128)S(1)}, u32[]{:S(2)}, u32[]{:S(2)}) collective-permute-start(f32[24,1024]{1,0:T(8,128)S(1)} %add.20), channel_id=1, source_target_pairs={{0,128},{128,0},{1,129},{129,1},{2,130},{130,2},{3,131},{131,3},{4... | collective-permute-start | bytes 294920 | tf_op jit(solution)/shard_map/ppermute | solution.py:599
  116.0 1.4 collective-permute-start.2
  117.4 4.9 %collective-permute-start.3 = (f32[24,1024]{1,0:T(8,128)S(1)}, f32[24,1024]{1,0:T(8,128)S(1)}, u32[]{:S(2)}, u32[]{:S(2)}) collective-permute-start(f32[24,1024]{1,0:T(8,128)S(1)} %add.22), channel_id=1, source_target_pairs={{0,128},{128,0},{1,129},{129,1},{2,130},{130,2},{3,131},{131,3},{4... | collective-permute-start | bytes 294920 | tf_op jit(solution)/shard_map/ppermute | solution.py:599

commit v4 on v3

--- a/solution.py
+++ b/solution.py
@@ -132,8 +132,11 @@
 
 
 def delay_step(received_ref, delay):
-    summed = jnp.sum(received_ref[...].reshape(32, 8, LANES), axis=0)
+    rows = received_ref.shape[0]
+    summed = jnp.sum(received_ref[...].reshape(rows // 8, 8, LANES), axis=0)
     summed = summed[0:4] + summed[4:8]
+    if rows == 2 * CHANNELS:
+        summed = summed[0:2] + summed[2:4]
     step = DAMPING * summed[0:1] / summed[1:2]
     low = low_half((1, LANES))
     turned = half_roll(jnp.broadcast_to(step, (8, LANES)))[0:1]
@@ -319,17 +322,15 @@
 
 
 def split_into(left_ref, lanes, terms):
-    high = terms.astype(jnp.bfloat16)
-    rest = terms - high.astype(F32)
-    middle = rest.astype(jnp.bfloat16)
-    low = (rest - middle.astype(F32)).astype(jnp.bfloat16)
-    left_ref[0:48, lanes] = high
-    left_ref[48:96, lanes] = middle
-    left_ref[96:144, lanes] = low
+    for at in range(0, 6, 2):
+        pair = jnp.concatenate(terms[at : at + 2], axis=0)
+        high = pair.astype(jnp.bfloat16)
+        left_ref[at * 8 : at * 8 + 16, lanes] = high
+        left_ref[48 + at * 8 : 64 + at * 8, lanes] = (pair - high.astype(F32)).astype(jnp.bfloat16)
 
 
 def joined(sums):
-    return sums[0:48] + (sums[48:96] + sums[96:144])
+    return sums[0:48] + sums[48:96]
 
 
 def contract(left, right):
@@ -339,17 +340,14 @@
 def terms_of(pr, pi, qr, qi, cr, ci, power):
     rr = cr - (pr * qr + pi * qi) * power
     ri = ci - (pi * qr - pr * qi) * power
-    return jnp.concatenate(
-        [
-            qr * rr - qi * ri,
-            qr * ri + qi * rr,
-            (qr * qr + qi * qi) * power,
-            pr * rr + pi * ri,
-            pi * rr - pr * ri,
-            (pr * pr + pi * pi) * power,
-        ],
-        axis=0,
-    )
+    return [
+        qr * rr - qi * ri,
+        qr * ri + qi * rr,
+        (qr * qr + qi * qi) * power,
+        pr * rr + pi * ri,
+        pi * rr - pr * ri,
+        (pr * pr + pi * pi) * power,
+    ]
 
 
 def packed_sources(gr, gi):
@@ -500,7 +498,7 @@
                 (br * br + bi * bi) * ((pr * pr + pi * pi) * power),
             ]
             total = terms if total is None else [a + b for a, b in zip(total, terms)]
-        split_into(left_ref, pl.ds(inner * LANES, LANES), jnp.concatenate(total, axis=0))
+        split_into(left_ref, pl.ds(inner * LANES, LANES), total)
     sums = joined(contract(left_ref[...], hot_ref[...]))
     row = lax.broadcasted_iota(jnp.int32, (8, LANES), 0)
     chosen = [
@@ -551,7 +549,7 @@
 
 
 def solve_kernel(
-    mix_ref, index_ref, hot_ref, band_ref, delay_ref, own_ref, new_ref, send_ref, left_ref
+    riding, mix_ref, index_ref, hot_ref, band_ref, delay_ref, own_ref, new_ref, send_ref, left_ref
 ):
     x = own_offset(own_ref)
     angle = TURN * delay_ref[...] * x
@@ -568,8 +566,9 @@
     n = turning * (hr * ui - hi * ur)
     d = (turning * turning) * ((hr * hr + hi * hi) * w)
     low = low_half((1, LANES))
-    four = [jnp.where(low, p[0:1], p[1:2]) for p in (n, d, band[0:2], band[2:4])]
-    copies(jnp.concatenate(four * 2, axis=0), send_ref)
+    sent = [n, d] + ([band[0:2], band[2:4]] if riding else [])
+    sent = [jnp.where(low, part[0:1], part[1:2]) for part in sent]
+    copies(jnp.concatenate(sent * (8 // len(sent)), axis=0), send_ref)
 
 
 def call(body, outs, operands, scratch=()):
@@ -645,8 +644,8 @@
         ),
     )
     group = exchange(data, YX)
-    wide = pltpu.VMEM((144, 2 * LANES), jnp.bfloat16)
-    half_wide = pltpu.VMEM((144, padded // 2), jnp.bfloat16)
+    wide = pltpu.VMEM((96, 2 * LANES), jnp.bfloat16)
+    half_wide = pltpu.VMEM((96, padded // 2), jnp.bfloat16)
     tall, short = pltpu.VMEM((32, LANES), F32), pltpu.VMEM((16, LANES), F32)
     for sweep in range(SWEEPS):
         if sweep == 0:
@@ -675,9 +674,10 @@
         gain, mix, *kept = call(
             mix_kernel, outs, (data, exchange(send, FREQ), index, gain), scratch
         )
+        riding = sweep < SWEEPS - 1
         band, send = call(
-            solve_kernel,
-            [rows(4), rows(256)],
+            functools.partial(solve_kernel, riding),
+            [rows(4), rows((4 if riding else 2) * channels)],
             (pair_total(mix), index, hot, band, delay, own),
             (half_wide,),
         )

time: 143 us -> 143 us (level)
  no operation moved by 1% of the time
where the time goes in v4:
time: 143 us; the launch traced here: 142 us
  blocking collectives  120 us (84%)
  waiting for transfers between devices  9.42 us (7%)
  Pallas kernels  6.56 us (5%)
  starting transfers between devices  3.21 us (2%)
  local copies, waits for them, and re-layouts  2.77 us (2%)
    all_to_all x7, blocking collectives, exchange(): return lax.all_to_all(chunks, axis, 0, 0, tiled=True).reshape(array.shape)  120 us
    ppermute x4, waiting for transfers between devices, pair_total(): array = array + lax.ppermute(array, axis, [(0, 1), (1, 0)])  9.42 us
    pallas_call x10, Pallas kernels, call(): pl.pallas_call(body, out_shape=tuple((o if isinstance(o, jax.ShapeDtypeSt...  6.56 us
    ppermute x4, starting transfers between devices, pair_total(): array = array + lax.ppermute(array, axis, [(0, 1), (1, 0)])  3.21 us
  transfers between devices with their start and end apart: 4, of which 4 were waited for; matrix products, arithmetic and copies ran while one was open for 0% of the time, Pallas kernels for 0%

profile of v4, /device:TPU:2, one launch (start us, length us, event | category | flops | bytes accessed | tf_op | source)
XLA Modules:
  0.0 142.4 jit_solution(10624663950412543868)
XLA Ops:
  0.7 1.3 copy.21
  2.4 23.6 %all_to_all.35 = f32[8,1,33792]{2,1,0:T(1,128)S(1)} all-to-all(f32[8,1,33792]{2,1,0:T(1,128)S(1)} %bitcast.25), channel_id=1, replica_groups=mesh['tm_0'=2,'tm_1'=2,'freq_0'=4,'freq_1'=2,'freq_2'=8] {'freq_0','freq..., dimensions={0} | all-to-all | bytes 2162688 | tf_op jit(solution)/shard_map/all_to_all | solution.py:593
  26.0 0.4 shard_map.111
  26.4 16.6 %all_to_all.36 = f32[8,1,2048]{2,1,0:T(1,128)S(1)} all-to-all(f32[8,1,2048]{2,1,0:T(1,128)S(1)} %bitcast.40), channel_id=1, replica_groups=mesh['tm_0'=2,'tm_1'=2,'freq_0'=4,'freq_1'=2,'freq_2'=8] {'freq_2'}, dimensions={0} | all-to-all | bytes 131072 | tf_op jit(solution)/shard_map/all_to_all | solution.py:593
  43.1 0.6 shard_map.112
  43.7 17.5 %all_to_all.37 = f32[64,1,1024]{2,1,0:T(1,128)S(1)} all-to-all(f32[64,1,1024]{2,1,0:T(1,128)S(1)} %bitcast.29), channel_id=1, replica_groups=mesh['tm_0'=2,'tm_1'=2,'freq_0'=4,'freq_1'=2,'freq_2'=8] {'freq_0','freq..., dimensions={0} | all-to-all | bytes 524288 | tf_op jit(solution)/shard_map/all_to_all | solution.py:593
  61.2 0.3 shard_map.113
  61.6 1.3 collective-permute-done
  62.9 1.5 %collective-permute-start.1 = (f32[24,1024]{1,0:T(8,128)S(1)}, f32[24,1024]{1,0:T(8,128)S(1)}, u32[]{:S(2)}, u32[]{:S(2)}) collective-permute-start(f32[24,1024]{1,0:T(8,128)S(1)} %add.20), channel_id=1, source_target_pairs={{0,128},{128,0},{1,129},{129,1},{2,130},{130,2},{3,131},{131,3},{4... | collective-permute-start | bytes 294920 | tf_op jit(solution)/shard_map/ppermute | solution.py:598
  64.4 3.4 %collective-permute-done.1 = f32[24,1024]{1,0:T(8,128)S(1)} collective-permute-done((f32[24,1024]{1,0:T(8,128)S(1)}, f32[24,1024]{1,0:T(8,128)S(1)}, u32[]{:S(2)}, u32[]{:S(2)}) %collective-permute-start.1) | collective-permute-done | bytes 98336 | tf_op jit(solution)/shard_map/ppermute | solution.py:598
  67.8 1.3 shard_map.114
  69.1 17.1 %all_to_all.38 = f32[64,1,512]{2,1,0:T(1,128)S(1)} all-to-all(f32[64,1,512]{2,1,0:T(1,128)S(1)} %bitcast.37), channel_id=1, replica_groups=mesh['tm_0'=2,'tm_1'=2,'freq_0'=4,'freq_1'=2,'freq_2'=8] {'freq_0','freq..., dimensions={0} | all-to-all | bytes 262144 | tf_op jit(solution)/shard_map/all_to_all | solution.py:593
  86.2 0.5 shard_map.115
  86.7 10.8 %all_to_all.39 = f32[8,1,2048]{2,1,0:T(1,128)S(1)} all-to-all(f32[8,1,2048]{2,1,0:T(1,128)S(1)} %bitcast.38), channel_id=1, replica_groups=mesh['tm_0'=2,'tm_1'=2,'freq_0'=4,'freq_1'=2,'freq_2'=8] {'freq_2'}, dimensions={0} | all-to-all | bytes 131072 | tf_op jit(solution)/shard_map/all_to_all | solution.py:593
  97.5 0.6 shard_map.116
  98.1 17.5 %all_to_all.40 = f32[64,1,1024]{2,1,0:T(1,128)S(1)} all-to-all(f32[64,1,1024]{2,1,0:T(1,128)S(1)} %bitcast.28), channel_id=1, replica_groups=mesh['tm_0'=2,'tm_1'=2,'freq_0'=4,'freq_1'=2,'freq_2'=8] {'freq_0','freq..., dimensions={0} | all-to-all | bytes 524288 | tf_op jit(solution)/shard_map/all_to_all | solution.py:593
  115.6 0.3 shard_map.117
  116.0 1.3 collective-permute-done.2
  117.3 1.5 %collective-permute-start.3 = (f32[24,1024]{1,0:T(8,128)S(1)}, f32[24,1024]{1,0:T(8,128)S(1)}, u32[]{:S(2)}, u32[]{:S(2)}) collective-permute-start(f32[24,1024]{1,0:T(8,128)S(1)} %add.22), channel_id=1, source_target_pairs={{0,128},{128,0},{1,129},{129,1},{2,130},{130,2},{3,131},{131,3},{4... | collective-permute-start | bytes 294920 | tf_op jit(solution)/shard_map/ppermute | solution.py:598
  118.8 3.4 %collective-permute-done.3 = f32[24,1024]{1,0:T(8,128)S(1)} collective-permute-done((f32[24,1024]{1,0:T(8,128)S(1)}, f32[24,1024]{1,0:T(8,128)S(1)}, u32[]{:S(2)}, u32[]{:S(2)}) %collective-permute-start.3) | collective-permute-done | bytes 98336 | tf_op jit(solution)/shard_map/ppermute | solution.py:598
  122.2 1.3 shard_map.118
  123.5 16.5 %all_to_all.41 = f32[64,1,256]{2,1,0:T(1,128)S(1)} all-to-all(f32[64,1,256]{2,1,0:T(1,128)S(1)} %bitcast.39), channel_id=1, replica_groups=mesh['tm_0'=2,'tm_1'=2,'freq_0'=4,'freq_1'=2,'freq_2'=8] {'freq_0','freq..., dimensions={0} | all-to-all | bytes 131072 | tf_op jit(solution)/shard_map/all_to_all | solution.py:593
  140.1 1.0 shard_map.119
  141.1 1.3 copy.20
  (20 shorter events, 0.7 us)
Async XLA Ops:
  0.6 1.3 copy-start.5
  0.6 1.5 %copy-start.1 = (s32[2016]{0:T(1024)S(1)}, s32[2016]{0:T(1024)}, u32[]{:S(2)}) copy-start(s32[2016]{0:T(1024)} %param.13) | copy-start | bytes 24196
  0.7 1.5 %copy-start = (s32[2016]{0:T(1024)S(1)}, s32[2016]{0:T(1024)}, u32[]{:S(2)}) copy-start(s32[2016]{0:T(1024)} %param.12) | copy-start | bytes 24196
  0.7 1.5 %copy-start.4 = (f32[2,64]{1,0:T(2,128)S(1)}, f32[2,64]{1,0:T(2,128)}, u32[]{:S(2)}) copy-start(f32[2,64]{1,0:T(2,128)} %refs_4_.1) | copy-start | bytes 1540
  0.7 1.5 %copy-start.3 = (f32[2,2,1,64]{3,2,1,0:T(1,128)S(1)}, f32[2,2,1,64]{3,2,1,0:T(1,128)}, u32[]{:S(2)}) copy-start(f32[2,2,1,64]{3,2,1,0:T(1,128)} %refs_3_.1) | copy-start | bytes 3076
  0.7 1.5 %copy-start.2 = (f32[2,2,2,64]{3,2,1,0:T(2,128)S(1)}, f32[2,2,2,64]{3,2,1,0:T(2,128)}, u32[]{:S(2)}) copy-start(f32[2,2,2,64]{3,2,1,0:T(2,128)} %refs_2_.1) | copy-start | bytes 6148
  61.5 1.4 collective-permute-start
  62.9 4.9 %collective-permute-start.1 = (f32[24,1024]{1,0:T(8,128)S(1)}, f32[24,1024]{1,0:T(8,128)S(1)}, u32[]{:S(2)}, u32[]{:S(2)}) collective-permute-start(f32[24,1024]{1,0:T(8,128)S(1)} %add.20), channel_id=1, source_target_pairs={{0,128},{128,0},{1,129},{129,1},{2,130},{130,2},{3,131},{131,3},{4... | collective-permute-start | bytes 294920 | tf_op jit(solution)/shard_map/ppermute | solution.py:598
  115.9 1.4 collective-permute-start.2
  117.3 4.9 %collective-permute-start.3 = (f32[24,1024]{1,0:T(8,128)S(1)}, f32[24,1024]{1,0:T(8,128)S(1)}, u32[]{:S(2)}, u32[]{:S(2)}) collective-permute-start(f32[24,1024]{1,0:T(8,128)S(1)} %add.22), channel_id=1, source_target_pairs={{0,128},{128,0},{1,129},{129,1},{2,130},{130,2},{3,131},{131,3},{4... | collective-permute-start | bytes 294920 | tf_op jit(solution)/shard_map/ppermute | solution.py:598
